TPU v7x, 32 devices: a whole 2x2x4 slice. The times are simulated.
32 devices in a mesh: head: 2 (over y), blk: 16 (over z, x, core).
Axes of the slice: x: 2, y: 2, z: 4, core: 2. Of those that a mesh axis runs over, the one named last changes fastest.
Arguments:
- tokens: bfloat16 [2, 2, 1024, 767], P(None, 'head', 'blk'), may hold values from -6 to 6
- segments: int32 [2, 2, 1024], P(None, 'head', 'blk'), may hold values from 0 to 8, as said below
- cotangent: bfloat16 [2, 2, 1024, 767], P(None, 'head', 'blk'), may hold values from -6 to 6
- w_qkv: bfloat16 [768, 2304], P(('head', 'blk')), may hold values from -0.21875 to 0.21875
- w_out: bfloat16 [768, 767], P(('head', 'blk')), may hold values from -1.75 to 1.75
- w_up: bfloat16 [768, 3072], P(('head', 'blk')), may hold values from -0.21875 to 0.21875
- w_down: bfloat16 [3072, 767], P(('head', 'blk')), may hold values from -0.109375 to 0.109375
- gain_one: bfloat16 [768], P(('head', 'blk')), may hold values from 0.5 to 1.5
- gain_two: bfloat16 [768], P(('head', 'blk')), may hold values from 0.5 to 1.5
Outputs:
- mixed: bfloat16 [2, 2, 1024, 767], P(None, 'head', 'blk')
- grad_tokens: float32 [2, 2, 1024, 767], P(None, 'head', 'blk')
- grad_w_qkv: float32 [768, 2304], P(('head', 'blk'))
- grad_w_out: float32 [768, 767], P(('head', 'blk'))
- grad_w_up: float32 [768, 3072], P(('head', 'blk'))
- grad_w_down: float32 [3072, 767], P(('head', 'blk'))
- grad_gain_one: float32 [768], P(('head', 'blk'))
- grad_gain_two: float32 [768], P(('head', 'blk'))
Inputs may be any that keep to these rules, and one draw needn't show every extreme that they name: `segments`: in each group positions 0 to 511 carry 0; later positions carry 1 to 8, never falling, every continuation 1024 // 32 positions or more.
All inputs are finite; a program needn't handle non-finite values.
Results may differ from a plain program's by a relative error of at most 0.039.
Values may be sent and summed in bfloat16 or wider, within the bound.
No kernel may reach another device: no remote copies, remote signals or barrier semaphores. Data moves between devices by JAX's collectives and lax.ppermute only.
A program may use at most 384 MiB of HBM per device.

v0:
```python
import math

import jax
import jax.numpy as jnp
from jax import lax
from jax.experimental import pallas as pl
from jax.experimental.pallas import tpu as pltpu
from jax.sharding import PartitionSpec as P

HEAD_DIM = 64


def compress_norm(values, gain):
    total_sum = jnp.sum(values, axis=-1, keepdims=True)
    full_vec = jnp.concatenate([values, -total_sum], axis=-1)
    factor = lax.rsqrt(jnp.mean(full_vec * full_vec, axis=-1, keepdims=True) + 1e-05)
    return full_vec * factor * gain


def gelu_tanh(values):
    return jax.nn.gelu(values, approximate=True)


def visibility(query_pos, query_seg, key_pos, key_seg):
    causal = key_pos[:, None, :] <= query_pos[None, :, None]
    shared = (key_seg[:, None, :] == 0) | (key_seg[:, None, :] == query_seg[:, :, None])
    return (causal & shared)[:, :, None, :]


def micro_step(token_block, segment_block, cotangent_block, weights_full, query_pos):
    proj_qkv, proj_out, proj_up, proj_down, norm_one, norm_two = weights_full
    norm_one = norm_one.astype(jnp.float32)
    norm_two = norm_two.astype(jnp.float32)
    group_local, seg_len, resid_width = token_block.shape
    model_width = proj_qkv.shape[0]
    row_count = group_local * seg_len
    score_scale = 1.0 / math.sqrt(HEAD_DIM)
    token_rows = token_block.astype(jnp.float32).reshape(row_count, resid_width)
    normed_f, norm_one_pull = jax.vjp(compress_norm, token_rows, norm_one)
    normed_one = normed_f.astype(jnp.bfloat16)
    projected = jnp.dot(normed_one, proj_qkv, preferred_element_type=jnp.float32).astype(
        jnp.bfloat16
    )
    projected = projected.reshape(group_local, seg_len, 3, model_width)
    head_groups = lax.axis_size("head")
    seg_wide = jnp.broadcast_to(
        segment_block.astype(jnp.bfloat16)[:, :, None, None], (group_local, seg_len, 1, head_groups)
    )
    moved_qkv, moved_seg = (
        lax.all_to_all(projected, "head", split_axis=3, concat_axis=0, tiled=True),
        lax.all_to_all(seg_wide, "head", split_axis=3, concat_axis=0, tiled=True),
    )
    groups = moved_qkv.shape[0]
    head_width = moved_qkv.shape[3]
    heads_here = head_width // HEAD_DIM
    head_shape = (groups, seg_len, heads_here, HEAD_DIM)
    queries = moved_qkv[:, :, 0].reshape(head_shape)
    keys_flat = moved_qkv[:, :, 1]
    values_flat = moved_qkv[:, :, 2]
    keys_local = keys_flat.reshape(head_shape)
    values_local = values_flat.reshape(head_shape)
    seg_bf = moved_seg[:, :, 0, 0]
    seg_here = seg_bf.astype(jnp.int32)
    key_piece = lax.all_gather(keys_flat, "blk", axis=1, tiled=True)
    value_piece = lax.all_gather(values_flat, "blk", axis=1, tiled=True)
    seg_piece = lax.all_gather(seg_bf, "blk", axis=1, tiled=True)
    key_pos = jnp.arange(key_piece.shape[1], dtype=jnp.int32)[None, :]
    running_max = jnp.full((groups, seg_len, heads_here), -1e30, jnp.float32)
    piece_rows = key_piece.shape[1]
    visible = visibility(query_pos, seg_here, key_pos, seg_piece.astype(jnp.int32))
    key_heads = key_piece.reshape(groups, piece_rows, heads_here, HEAD_DIM)
    value_heads = value_piece.reshape(groups, piece_rows, heads_here, HEAD_DIM)
    scores = score_scale * jnp.einsum(
        "gqhd,gkhd->gqhk", queries, key_heads, preferred_element_type=jnp.float32
    )
    masked = jnp.where(visible, scores, -1e30)
    new_max = jnp.maximum(running_max, jnp.max(masked, axis=-1))
    exp_terms = jnp.where(visible, jnp.exp(masked - new_max[..., None]), 0.0)
    new_sum = jnp.sum(exp_terms, axis=-1)
    new_acc = jnp.einsum(
        "gqhk,gkhd->gqhd",
        exp_terms.astype(jnp.bfloat16),
        value_heads,
        preferred_element_type=jnp.float32,
    )
    attn_f = new_acc / new_sum[..., None]
    log_totals = new_max + jnp.log(new_sum)
    attn_heads = attn_f.astype(jnp.bfloat16).reshape(groups, seg_len, head_width)
    attention = lax.all_to_all(attn_heads, "head", split_axis=0, concat_axis=2, tiled=True)
    attn_rows = attention.reshape(row_count, model_width)
    residual = token_rows + jnp.dot(attn_rows, proj_out, preferred_element_type=jnp.float32)
    normed_two_f, norm_two_pull = jax.vjp(compress_norm, residual, norm_two)
    normed_two = normed_two_f.astype(jnp.bfloat16)
    hidden = jnp.dot(normed_two, proj_up, preferred_element_type=jnp.float32)
    activated_f, gelu_pull = jax.vjp(gelu_tanh, hidden)
    activated = activated_f.astype(jnp.bfloat16)
    mixed = (residual + jnp.dot(activated, proj_down, preferred_element_type=jnp.float32)).astype(
        jnp.bfloat16
    )
    cot_rows = cotangent_block.reshape(row_count, resid_width)
    grad_down = jnp.einsum("ra,rb->ab", activated, cot_rows, preferred_element_type=jnp.float32)
    d_activated = jnp.einsum("rb,ab->ra", cot_rows, proj_down, preferred_element_type=jnp.float32)
    (d_hidden,) = gelu_pull(d_activated)
    d_hidden = d_hidden.astype(jnp.bfloat16)
    grad_up = jnp.einsum("ra,rb->ab", normed_two, d_hidden, preferred_element_type=jnp.float32)
    d_normed_two = jnp.einsum("rb,ab->ra", d_hidden, proj_up, preferred_element_type=jnp.float32)
    d_resid_part, grad_gain_two = norm_two_pull(d_normed_two)
    d_residual = cot_rows.astype(jnp.float32) + d_resid_part
    d_sum = d_residual.astype(jnp.bfloat16)
    grad_out = jnp.einsum("ra,rb->ab", attn_rows, d_sum, preferred_element_type=jnp.float32)
    d_attention = jnp.einsum(
        "rb,ab->ra", d_sum, proj_out, preferred_element_type=jnp.float32
    ).astype(jnp.bfloat16)
    d_attention = d_attention.reshape(group_local, seg_len, model_width)
    d_heads_flat = lax.all_to_all(d_attention, "head", split_axis=2, concat_axis=0, tiled=True)
    d_heads = d_heads_flat.reshape(head_shape)
    delta_rows = jnp.sum(d_heads.astype(jnp.float32) * attn_f, axis=-1)
    lse_all, delta_all = (
        lax.all_gather(log_totals, "blk", axis=1, tiled=True),
        lax.all_gather(delta_rows, "blk", axis=1, tiled=True),
    )
    key_piece = lax.all_gather(keys_flat, "blk", axis=1, tiled=True)
    value_piece = lax.all_gather(values_flat, "blk", axis=1, tiled=True)
    seg_piece = lax.all_gather(seg_bf, "blk", axis=1, tiled=True)
    key_pos = jnp.arange(key_piece.shape[1], dtype=jnp.int32)[None, :]
    piece_rows = key_piece.shape[1]
    visible = visibility(query_pos, seg_here, key_pos, seg_piece.astype(jnp.int32))
    key_heads = key_piece.reshape(groups, piece_rows, heads_here, HEAD_DIM)
    value_heads = value_piece.reshape(groups, piece_rows, heads_here, HEAD_DIM)
    scores = score_scale * jnp.einsum(
        "gqhd,gkhd->gqhk", queries, key_heads, preferred_element_type=jnp.float32
    )
    masked = jnp.where(visible, scores, -1e30)
    soft_weights = jnp.where(visible, jnp.exp(masked - log_totals[..., None]), 0.0)
    d_soft = jnp.einsum("gqhd,gkhd->gqhk", d_heads, value_heads, preferred_element_type=jnp.float32)
    d_scores = (soft_weights * (d_soft - delta_rows[..., None])).astype(jnp.bfloat16)
    d_query = score_scale * jnp.einsum(
        "gqhk,gkhd->gqhd", d_scores, key_heads, preferred_element_type=jnp.float32
    )
    queries_flat = moved_qkv[:, :, 0]
    query_piece = lax.all_gather(queries_flat, "blk", axis=1, tiled=True)
    dout_piece = lax.all_gather(d_heads_flat, "blk", axis=1, tiled=True)
    seg_piece = lax.all_gather(seg_bf, "blk", axis=1, tiled=True)
    piece_rows = query_piece.shape[1]
    piece_pos = jnp.arange(piece_rows, dtype=jnp.int32)
    visible = visibility(piece_pos, seg_piece.astype(jnp.int32), query_pos[None, :], seg_here)
    query_heads = query_piece.reshape(groups, piece_rows, heads_here, HEAD_DIM)
    dout_heads = dout_piece.reshape(groups, piece_rows, heads_here, HEAD_DIM)
    scores = score_scale * jnp.einsum(
        "gqhd,gkhd->gqhk", query_heads, keys_local, preferred_element_type=jnp.float32
    )
    masked = jnp.where(visible, scores, -1e30)
    soft_weights = jnp.where(visible, jnp.exp(masked - lse_all[..., None]), 0.0)
    d_soft = jnp.einsum(
        "gqhd,gkhd->gqhk", dout_heads, values_local, preferred_element_type=jnp.float32
    )
    d_scores = (soft_weights * (d_soft - delta_all[..., None])).astype(jnp.bfloat16)
    new_value = jnp.einsum(
        "gqhk,gqhd->gkhd",
        soft_weights.astype(jnp.bfloat16),
        dout_heads,
        preferred_element_type=jnp.float32,
    )
    new_key = score_scale * jnp.einsum(
        "gqhk,gqhd->gkhd", d_scores, query_heads, preferred_element_type=jnp.float32
    )
    d_stacked = (
        jnp.stack([d_query, new_key, new_value], axis=2)
        .astype(jnp.bfloat16)
        .reshape(groups, seg_len, 3, head_width)
    )
    d_projected = lax.all_to_all(d_stacked, "head", split_axis=0, concat_axis=3, tiled=True)
    d_proj_rows = d_projected.reshape(row_count, 3 * model_width)
    grad_qkv = jnp.einsum("ra,rb->ab", normed_one, d_proj_rows, preferred_element_type=jnp.float32)
    d_normed_one = jnp.einsum(
        "rb,ab->ra", d_proj_rows, proj_qkv, preferred_element_type=jnp.float32
    )
    d_token_part, grad_gain_one = norm_one_pull(d_normed_one)
    grad_tokens = (d_residual + d_token_part).reshape(group_local, seg_len, resid_width)
    mixed = mixed.reshape(group_local, seg_len, resid_width)
    return (
        mixed,
        grad_tokens,
        (grad_qkv, grad_out, grad_up, grad_down, grad_gain_one, grad_gain_two),
    )


def on_device(tokens, segments, cotangent, w_qkv, w_out, w_up, w_down, gain_one, gain_two):
    micro_count = tokens.shape[0]
    seg_len = tokens.shape[2]
    query_pos = lax.axis_index("blk") * seg_len + jnp.arange(seg_len, dtype=jnp.int32)
    mixed_list = []
    token_grad_list = []
    grad_terms = []
    for batch_index in range(micro_count):
        weights_full = (
            lax.all_gather(w_qkv, ("head", "blk"), axis=0, tiled=True),
            lax.all_gather(w_out, ("head", "blk"), axis=0, tiled=True),
            lax.all_gather(w_up, ("head", "blk"), axis=0, tiled=True),
            lax.all_gather(w_down, ("head", "blk"), axis=0, tiled=True),
            lax.all_gather(gain_one, ("head", "blk"), axis=0, tiled=True),
            lax.all_gather(gain_two, ("head", "blk"), axis=0, tiled=True),
        )
        mixed, grad_tokens, gradients = micro_step(
            tokens[batch_index],
            segments[batch_index],
            cotangent[batch_index],
            weights_full,
            query_pos,
        )
        mixed_list.append(mixed)
        token_grad_list.append(grad_tokens)
        grad_terms.append(
            (
                lax.psum_scatter(gradients[0], ("head", "blk"), scatter_dimension=0, tiled=True),
                lax.psum_scatter(gradients[1], ("head", "blk"), scatter_dimension=0, tiled=True),
                lax.psum_scatter(gradients[2], ("head", "blk"), scatter_dimension=0, tiled=True),
                lax.psum_scatter(gradients[3], ("head", "blk"), scatter_dimension=0, tiled=True),
                lax.psum_scatter(gradients[4], ("head", "blk"), scatter_dimension=0, tiled=True),
                lax.psum_scatter(gradients[5], ("head", "blk"), scatter_dimension=0, tiled=True),
            )
        )
    summed = grad_terms[0]
    for later_terms in grad_terms[1:]:
        summed = tuple((first + second for first, second in zip(summed, later_terms)))
    mixed_all = jnp.stack(mixed_list, axis=0)
    token_grads = jnp.stack(token_grad_list, axis=0)
    return (
        mixed_all,
        token_grads,
        summed[0],
        summed[1],
        summed[2],
        summed[3],
        summed[4],
        summed[5],
    )


CORE, AXIS_X, AXIS_Z_NEAR, AXIS_Z_FAR, AXIS_Y = 1, 2, 4, 8, 16
DEVICES = 32
WIDTH = 768
HALF = 384
UNITS = 1536
ROWS = 256
POSITIONS = 1024
MIB = 1024 * 1024


def swap(array, bit, keep=lambda source: True):
    pairs = [(i, i ^ bit) for i in range(DEVICES) if keep(i)]
    return lax.ppermute(array, ("head", "blk"), pairs)


def upward(bit):
    return lambda source: source & bit == 0


def downward(bit):
    return lambda source: source & bit != 0


def dot(a, b):
    return lax.dot_general(a, b, (((1,), (0,)), ((), ())), preferred_element_type=jnp.float32)


def dot_nt(a, b):
    return lax.dot_general(a, b, (((1,), (1,)), ((), ())), preferred_element_type=jnp.float32)


def dot_tn(a, b):
    return lax.dot_general(a, b, (((0,), (0,)), ((), ())), preferred_element_type=jnp.float32)


def lanes(rows):
    return lax.broadcasted_iota(jnp.int32, (rows, WIDTH), 1)


def norm_rows(values, lane):
    inner = jnp.where(lane < WIDTH - 1, values, 0.0)
    total = jnp.sum(inner, axis=-1, keepdims=True)
    full = jnp.where(lane == WIDTH - 1, -total, inner)
    factor = lax.rsqrt(jnp.mean(full * full, axis=-1, keepdims=True) + 1e-05)
    return full * factor, factor


def norm_rows_back(d_normed, normed, factor, lane):
    inner = jnp.mean(d_normed * normed, axis=-1, keepdims=True)
    d_full = factor * (d_normed - normed * inner)
    last = jnp.sum(jnp.where(lane == WIDTH - 1, d_full, 0.0), axis=-1, keepdims=True)
    return jnp.where(lane < WIDTH - 1, d_full - last, 0.0)


def piece_chip(which, pair, entry):
    z_bits = (entry & 3) << 1
    other = entry >> 2
    return z_bits | ((other | pair << 3) if which == 0 else (other << 3 | pair))


def gather_z(block):
    near = swap(block, AXIS_Z_NEAR)
    far = swap(block, AXIS_Z_FAR)
    end = swap(block, AXIS_Z_NEAR | AXIS_Z_FAR)
    return block, near, far, end


def gather_first(four, cut):
    four_a = jnp.stack([array[:, :cut] for array in four])
    four_b = jnp.stack([array[:, cut:] for array in four])
    return four_a, swap(four_a, AXIS_X), four_b, swap(four_b, AXIS_Y)


def gather_second(four_a, got_a, four_b, got_b):
    eight_a = jnp.concatenate([four_a, got_a], axis=0)
    eight_b = jnp.concatenate([four_b, got_b], axis=0)
    return eight_a, swap(eight_a, AXIS_Y), eight_b, swap(eight_b, AXIS_X)


def add(first, *others):
    total = first.astype(jnp.float32)
    for other in others:
        total = total + other.astype(jnp.float32)
    return total


def reduce_start(pieces):
    keep_a, send_a, keep_b, send_b = pieces
    return keep_a, swap(send_a, AXIS_Y), keep_b, swap(send_b, AXIS_X)


def reduce_middle(keep_a, got_a, keep_b, got_b):
    send_a = add(keep_a[4:], got_a[4:]).astype(jnp.bfloat16)
    send_b = add(keep_b[4:], got_b[4:]).astype(jnp.bfloat16)
    left_a = (keep_a[:4], got_a[:4], swap(send_a, AXIS_X))
    left_b = (keep_b[:4], got_b[:4], swap(send_b, AXIS_Y))
    return left_a, left_b


def along_z(four):
    near = swap(four[1], AXIS_Z_NEAR)
    far = swap(four[2], AXIS_Z_FAR)
    end = swap(four[3], AXIS_Z_NEAR | AXIS_Z_FAR)
    return near, far, end


def reduce_z(left_a, left_b):
    four = jnp.concatenate([add(*left_a), add(*left_b)], axis=-1).astype(jnp.bfloat16)
    return (four[0], *along_z(four))


def fence(*arrays):
    return lax.optimization_barrier(arrays)


def piece_rows(chip, which, pair, entry):
    return pl.ds(pl.multiple_of((chip ^ piece_chip(which, pair, entry)) * 48, 16), 48)


def take_pieces(pieces, target, chip, which):
    def move(entry, carry):
        for pair in range(2):
            target[piece_rows(chip, which, pair, entry), :] = pieces[pair][entry]
        return carry

    lax.fori_loop(0, 8, move, 0)


def give_pieces(pieces, source, chip, which):
    def move(entry, carry):
        for pair in range(2):
            pieces[pair][entry] = source[piece_rows(chip, which, pair, entry), :]
        return carry

    lax.fori_loop(0, 8, move, 0)


def row_block(entry, place, core):
    rel = (entry & 3) << 1 | entry >> 2
    return pl.ds(pl.multiple_of(((place ^ rel) * 2 + core) * 64, 64), 64)


def split_heads(both):
    small = lax.broadcasted_iota(jnp.int32, both.shape, 1) < HEAD_DIM
    zero = jnp.zeros_like(both)
    return jnp.concatenate([jnp.where(small, both, zero), jnp.where(small, zero, both)], axis=0)


def join_heads(stacked):
    rows = stacked.shape[0] // 2
    small = lax.broadcasted_iota(jnp.int32, (rows, stacked.shape[1]), 1) < HEAD_DIM
    return jnp.where(small, stacked[:rows], stacked[rows:])


def forward_kernel(
    ids, tok_mine, tok_other, w0, w1, w2, w3,
    attn_out, query_out, own_out, gains_out, kv, normed, soft, wqkv, wout,
    tok, bias,
):
    chip, core = ids[0], ids[1]
    place = lax.rem(chip, 8)
    take_pieces((w0, w1), wqkv, chip, 0)
    take_pieces((w2, w3), wout, chip, 1)
    first_row = pl.multiple_of(place * 128, 128)
    lane = lanes(ROWS)
    picks = lax.broadcasted_iota(jnp.int32, (8, 128), 0) == lax.broadcasted_iota(
        jnp.int32, (8, 128), 1
    )
    gains_out[...] = dot_nt(picks.astype(jnp.bfloat16), wqkv[:, 3 * HALF :])
    gain = gains_out[0:1, :]
    for micro in range(2):
        def move(entry, carry, micro=micro):
            tok[micro, row_block(entry, place, core), :] = tok_mine[entry, micro]
            tok[micro, row_block(entry, place, 1 - core), :] = tok_other[entry, micro]
            return carry

        lax.fori_loop(0, 8, move, 0)

        def norm_chunk(chunk, carry, micro=micro):
            rows = pl.ds(pl.multiple_of(chunk * ROWS, ROWS), ROWS)
            values = tok[micro, rows, :].astype(jnp.float32)
            rows_normed = (norm_rows(values, lane)[0] * gain).astype(jnp.bfloat16)
            normed[micro, rows, :] = rows_normed
            kv[micro, rows, :] = dot(rows_normed, wqkv[:, HALF : 3 * HALF]).astype(jnp.bfloat16)
            return carry

        lax.fori_loop(0, POSITIONS // ROWS, norm_chunk, 0)
    hot = (lax.broadcasted_iota(jnp.int32, (8, WIDTH), 1) == WIDTH - 1).astype(jnp.bfloat16)
    for micro in range(2):
        here = slice(micro * 128, micro * 128 + 128)
        own = tok[micro, pl.ds(first_row, 128), :]
        own_out[here, :] = own
        query = dot(normed[micro, pl.ds(first_row, 128), :], wqkv[:, :HALF])
        query = query.astype(jnp.bfloat16) * jnp.bfloat16(0.125)
        query_out[here, :] = query
        query_seg = dot_nt(hot, own)[0:1, :]
        key_seg = tok[micro, :, WIDTH - 1 :].astype(jnp.float32)
        key_pos = lax.broadcasted_iota(jnp.int32, (POSITIONS, 128), 0)
        query_pos = first_row + lax.broadcasted_iota(jnp.int32, (POSITIONS, 128), 1)
        seen = (key_pos <= query_pos) & ((key_seg == 0.0) | (key_seg == query_seg))
        one = jnp.where(seen, 0.0, -1e30)
        bias[:, :128] = one
        bias[:, 128:] = one
        for pair in range(3):
            cols = slice(pair * 128, pair * 128 + 128)
            stacked = split_heads(query[:, cols])
            scores = dot_nt(kv[micro, :, cols], stacked) + bias[...]
            top = jnp.max(scores, axis=0, keepdims=True)
            terms = jnp.exp(scores - top)
            total = jnp.sum(terms, axis=0, keepdims=True)
            weights = (terms * (1.0 / total)).astype(jnp.bfloat16)
            soft[micro * 3 + pair] = weights
            value = kv[micro, :, HALF + pair * 128 : HALF + pair * 128 + 128]
            mixed = dot_tn(value, weights)
            attn_out[here, cols] = join_heads(mixed.T).astype(jnp.bfloat16)


def feed_half(normed, cot, up, down, g_up, g_down):
    slope = math.sqrt(2.0 / math.pi)
    hidden = dot(normed, up[...])
    square = hidden * hidden
    wave = jnp.tanh(slope * hidden * (1.0 + 0.044715 * square))
    active = (0.5 * hidden * (1.0 + wave)).astype(jnp.bfloat16)
    grow = 0.5 * (1.0 + wave) + 0.5 * hidden * (1.0 - wave * wave) * slope * (
        1.0 + 3.0 * 0.044715 * square
    )
    d_hidden = (dot_nt(cot, down[...]) * grow).astype(jnp.bfloat16)
    g_up[...] = dot_tn(normed, d_hidden).astype(jnp.bfloat16)
    g_down[...] = dot_tn(active, cot).astype(jnp.bfloat16)
    return dot(active, down[...]), dot_nt(d_hidden, up[...])


def feed_first_kernel(
    ids, gains, attn_mine, attn_other, own, wout_mine, wout_other, cot_mine, cot_other,
    w0, w1, w2, w3,
    attn_out, cot_out, res_out, normed_out, sum_mix, sum_norm, g0, g1, g2, g3,
    up, down, g_up, g_down,
):
    chip, core = ids[0], ids[1]
    take_pieces((w0, w1), up, chip, 0)
    take_pieces((w2, w3), down, chip, 1)
    mine_at = pl.multiple_of(core * HALF, 128)
    other_at = pl.multiple_of((1 - core) * HALF, 128)
    attn_out[:, pl.ds(mine_at, HALF)] = attn_mine[...]
    attn_out[:, pl.ds(other_at, HALF)] = attn_other[...]
    for micro in range(2):
        for side, source in ((core, cot_mine), (1 - core, cot_other)):
            at = pl.multiple_of(micro * 128 + side * 64, 64)
            cot_out[pl.ds(at, 64), :] = source[micro]
    lane = lanes(ROWS)
    attn = attn_out[...]
    res_out[:, pl.ds(mine_at, HALF)] = dot(attn, wout_mine[...])
    res_out[:, pl.ds(other_at, HALF)] = dot(attn, wout_other[...])
    own_values = jnp.where(lane < WIDTH - 1, own[...].astype(jnp.float32), 0.0)
    residual = res_out[...] + own_values
    res_out[...] = residual
    normed = (norm_rows(residual, lane)[0] * gains[1:2, :]).astype(jnp.bfloat16)
    normed_out[...] = normed
    mix, norm = feed_half(normed, cot_out[...], up, down, g_up, g_down)
    sum_mix[...] = mix
    sum_norm[...] = norm
    give_pieces((g0, g1), g_up, chip, 0)
    give_pieces((g2, g3), g_down, chip, 1)


def feed_second_kernel(
    ids, normed, cot, mix_in, norm_in, w0, w1, w2, w3,
    part_out, g0, g1, g2, g3,
    up, down, g_up, g_down,
):
    chip = ids[0]
    take_pieces((w0, w1), up, chip, 0)
    take_pieces((w2, w3), down, chip, 1)
    mix, norm = feed_half(normed[...], cot[...], up, down, g_up, g_down)
    part_out[:ROWS, :] = (mix_in[...] + mix).astype(jnp.bfloat16)
    part_out[ROWS:, :] = (norm_in[...] + norm).astype(jnp.bfloat16)
    give_pieces((g0, g1), g_up, chip, 0)
    give_pieces((g2, g3), g_down, chip, 1)


def backward_kernel(
    ids, gains, residual, part_mine, part_other, cot, wout_mine, wout_other, query,
    wqkv, kv, soft,
    mixed_out, dres_out, d_query, d_sum_half, keep_rows, send_rows, d_kv,
    d_attn, d_rows, d_sum_ref, hold,
):
    chip, core = ids[0], ids[1]
    place = lax.rem(chip, 8)
    first_row = pl.multiple_of(place * 128, 128)
    mine_at = pl.multiple_of(core * HALF, 128)
    other_at = pl.multiple_of((1 - core) * HALF, 128)
    lane = lanes(ROWS)
    res = residual[...]
    hold[...] = add(res, part_mine[:ROWS, :], part_other[:ROWS, :])
    for micro in range(2):
        at = pl.multiple_of(micro * 128 + core * 64, 64)
        mixed_out[micro] = hold[pl.ds(at, 64), : WIDTH - 1].astype(jnp.bfloat16)
    d_normed = add(part_mine[ROWS:, :], part_other[ROWS:, :]) * gains[1:2, :]
    normed_two, factor = norm_rows(res, lane)
    d_res = cot[...].astype(jnp.float32) + norm_rows_back(d_normed, normed_two, factor, lane)
    hold[...] = d_res
    for micro in range(2):
        at = pl.multiple_of(micro * 128 + core * 64, 64)
        dres_out[micro] = hold[pl.ds(at, 64), :]
    d_sum_ref[...] = d_res.astype(jnp.bfloat16)
    d_mine = d_sum_ref[:, pl.ds(mine_at, HALF)]
    d_other = d_sum_ref[:, pl.ds(other_at, HALF)]
    d_sum_half[...] = d_mine
    d_heads = dot_nt(d_mine, wout_mine[pl.ds(mine_at, HALF), :]) + dot_nt(
        d_other, wout_other[pl.ds(mine_at, HALF), :]
    )
    d_attn[...] = d_heads.astype(jnp.bfloat16)
    for micro in range(2):
        here = slice(micro * 128, micro * 128 + 128)
        for pair in range(3):
            cols = slice(pair * 128, pair * 128 + 128)
            value_cols = slice(HALF + pair * 128, HALF + pair * 128 + 128)
            d_out = split_heads(d_attn[here, cols])
            weights = soft[micro * 3 + pair]
            d_soft = dot_nt(kv[micro, :, value_cols], d_out)
            weights_f = weights.astype(jnp.float32)
            delta = jnp.sum(weights_f * d_soft, axis=0, keepdims=True)
            d_scores = (weights_f * (d_soft - delta)).astype(jnp.bfloat16)
            d_q = dot_tn(kv[micro, :, cols], d_scores) * 0.125
            d_query[here, cols] = join_heads(d_q.T).astype(jnp.bfloat16)
            d_kv[micro, :, cols] = dot(d_scores, split_heads(query[here, cols])).astype(
                jnp.bfloat16
            )
            d_kv[micro, :, value_cols] = dot(weights, d_out).astype(jnp.bfloat16)
        def row_chunk(chunk, carry, micro=micro):
            at = pl.ds(pl.multiple_of(chunk * ROWS, ROWS), ROWS)
            rows = dot_nt(d_kv[micro, at, :], wqkv[:, HALF : 3 * HALF])
            d_rows[micro, at, :] = rows.astype(jnp.bfloat16)
            return carry

        lax.fori_loop(0, POSITIONS // ROWS, row_chunk, 0)
        own = d_rows[micro, pl.ds(first_row, 128), :].astype(jnp.float32)
        own = own + dot_nt(d_query[here, :], wqkv[:, :HALF])
        d_rows[micro, pl.ds(first_row, 128), :] = own.astype(jnp.bfloat16)
        def part_rows(entry, carry, micro=micro):
            keep_rows[entry, micro] = d_rows[micro, row_block(entry, place, core), :]
            send_rows[entry, micro] = d_rows[micro, row_block(entry, place, 1 - core), :]
            return carry

        lax.fori_loop(0, 8, part_rows, 0)


def gradient_kernel(
    ids, attn, d_sum_half, d_query, d_kv, normed, g0, g1, g2, g3, g_a, g_b
):
    chip = ids[0]
    first_row = pl.multiple_of(lax.rem(chip, 8) * 128, 128)
    g_b[...] = dot_tn(attn[...], d_sum_half[...]).astype(jnp.bfloat16)
    own_0 = normed[0, pl.ds(first_row, 128), :]
    own_1 = normed[1, pl.ds(first_row, 128), :]
    g_a[:, :HALF] = (dot_tn(own_0, d_query[:128, :]) + dot_tn(own_1, d_query[128:, :])).astype(
        jnp.bfloat16
    )
    g_a[:, HALF:] = (dot_tn(normed[0], d_kv[0]) + dot_tn(normed[1], d_kv[1])).astype(jnp.bfloat16)
    give_pieces((g0, g1), g_a, chip, 0)
    give_pieces((g2, g3), g_b, chip, 1)


def tail_kernel(gains, tokens, d_0, d_1, d_2, d_3, d_residual, grad_out):
    lane = lanes(128)
    rows = (128, WIDTH)
    values = tokens[...].reshape(rows).astype(jnp.float32)
    normed, factor = norm_rows(values, lane)
    d_normed = add(d_0[...], d_1[...], d_2[...], d_3[...]).reshape(rows) * gains[0:1, :]
    out = d_residual[...].reshape(rows) + norm_rows_back(d_normed, normed, factor, lane)
    grad_out[...] = out[:, : WIDTH - 1].reshape(2, 64, WIDTH - 1)


VMEM = pl.BlockSpec(memory_space=pltpu.VMEM)
SMEM = pl.BlockSpec(memory_space=pltpu.SMEM)


def shaped(shape, dtype=jnp.bfloat16):
    return jax.ShapeDtypeStruct(shape, dtype)


def call(kernel, ins, outs, scratch, name, mib, flops=0, bytes_accessed=0):
    return pl.pallas_call(
        kernel,
        in_specs=[spec for spec in ins],
        out_specs=[spec for spec, _ in outs],
        out_shape=[shape for _, shape in outs],
        scratch_shapes=scratch,
        name=name,
        cost_estimate=pl.CostEstimate(
            flops=flops, transcendentals=0, bytes_accessed=bytes_accessed
        ),
        compiler_params=pltpu.CompilerParams(vmem_limit_bytes=mib * MIB),
    )


def pick(core, zero, one):
    return jnp.where(core == 0, zero, one)


def chip_block(core, for_zero, for_one):
    mine = pick(core, for_zero, for_one)
    other = swap(pick(core, for_one, for_zero), CORE)
    return jnp.concatenate([pick(core, mine, other), pick(core, other, mine)], axis=0)


def core_rows(core, block):
    rows = block.shape[0] // 2
    mine = pick(core, block[:rows], block[rows:])
    other = swap(pick(core, block[rows:], block[:rows]), CORE)
    return pick(core, mine, other), pick(core, other, mine)


def split_units(w_up, blocks):
    rows = w_up.shape[0]
    parts = w_up.reshape(rows, blocks, 2, 2, -1)
    return [parts[:, :, k].swapaxes(1, 2).reshape(rows, -1) for k in range(2)]


def join_units(first, second, blocks):
    rows = first.shape[0]
    parts = [half.reshape(rows, 2, blocks, -1).swapaxes(1, 2) for half in (first, second)]
    return jnp.stack(parts, axis=2).reshape(rows, -1)


def on_chip_pair(tokens, segments, cotangent, w_qkv, w_out, w_up, w_down, gain_one, gain_two):
    bf, f32 = jnp.bfloat16, jnp.float32
    device = lax.axis_index("head") * 16 + lax.axis_index("blk")
    core = device % 2
    ids = jnp.stack([device // 2, core]).astype(jnp.int32)
    own = jnp.concatenate([tokens[:, 0], segments[:, 0, :, None].astype(bf)], axis=-1)
    cot = jnp.pad(cotangent[:, 0], ((0, 0), (0, 0), (0, 1)))
    four = jnp.stack(
        [
            own,
            swap(own, AXIS_Z_NEAR, upward(AXIS_Z_NEAR)),
            swap(own, AXIS_Z_FAR, upward(AXIS_Z_FAR)),
            swap(own, AXIS_Z_NEAR | AXIS_Z_FAR, upward(AXIS_Z_FAR)),
        ]
    )
    got_x = swap(four, AXIS_X)
    eight = jnp.concatenate([four, got_x], axis=0)
    eight_other = swap(eight, CORE)
    gain_cols = jnp.pad(jnp.stack([gain_one, gain_two], axis=-1), ((0, 0), (0, 126)))
    out_wide = jnp.pad(w_out, ((0, 0), (0, 1)))
    down_wide = jnp.pad(w_down, ((0, 0), (0, 1)))
    qkv_parts = w_qkv.reshape(-1, 3, 2, HALF)
    attn_halves = [
        jnp.concatenate(
            [qkv_parts[:, 0, k], qkv_parts[:, 1, k], qkv_parts[:, 2, k], gain_cols]
            + [out_wide[:, k * HALF : k * HALF + HALF]],
            axis=-1,
        )
        for k in range(2)
    ]
    wide = 3 * HALF + 128
    attn_four = gather_z(chip_block(core, *attn_halves))
    attn_four = fence(*attn_four, got_x)[:4]
    attn_first = gather_first(attn_four, wide)
    up_block = chip_block(core, *split_units(w_up, 16))
    feed_blocks = [
        jnp.concatenate(
            [up_block[:, half * WIDTH :][:, :WIDTH], down_wide[half * 48 : half * 48 + 48]], axis=-1
        )
        for half in range(2)
    ]
    four_0 = gather_z(fence(feed_blocks[0], *attn_four[1:])[0])
    four_1 = gather_z(fence(feed_blocks[1], *four_0[1:])[0])
    attn_pieces = gather_second(*attn_first)
    first_0 = gather_first(fence(*four_0, *attn_first)[:4], WIDTH)
    first_1 = gather_first(fence(*four_1, *first_0)[:4], WIDTH)
    pieces_0 = gather_second(*first_0)
    cot_other = swap(cot, CORE)
    rows_shape = shaped((2, POSITIONS, WIDTH))
    attn, query, own_rows, gains, kv, normed_all, soft, wqkv, wout = call(
        forward_kernel,
        [SMEM] + [VMEM] * 6,
        [
            (VMEM, shaped((ROWS, HALF))),
            (VMEM, shaped((ROWS, HALF))),
            (VMEM, shaped((ROWS, WIDTH))),
            (VMEM, shaped((8, WIDTH), f32)),
            (VMEM, rows_shape),
            (VMEM, rows_shape),
            (VMEM, shaped((6, POSITIONS, ROWS))),
            (VMEM, shaped((WIDTH, wide))),
            (VMEM, shaped((WIDTH, HALF))),
        ],
        [
            pltpu.VMEM((2, POSITIONS, WIDTH), bf),
            pltpu.VMEM((POSITIONS, ROWS), f32),
        ],
        "attention_forward",
        30,
    )(ids, eight, eight_other, *attn_pieces)
    attn_other = swap(attn, CORE)
    wout_other = swap(wout, CORE)
    pieces_1 = gather_second(*first_1)
    weight_scratch = [pltpu.VMEM((WIDTH, WIDTH), bf)] * 4
    piece_shapes = [(VMEM, shaped((8, 48, WIDTH)))] * 4
    outs = call(
        feed_first_kernel,
        [SMEM] + [VMEM] * 8 + [VMEM] * 4,
        [
            (VMEM, shaped((ROWS, WIDTH))),
            (VMEM, shaped((ROWS, WIDTH))),
            (VMEM, shaped((ROWS, WIDTH), f32)),
            (VMEM, shaped((ROWS, WIDTH))),
            (VMEM, shaped((ROWS, WIDTH), f32)),
            (VMEM, shaped((ROWS, WIDTH), f32)),
        ]
        + piece_shapes,
        weight_scratch,
        "feed_forward_and_back_first",
        20,
    )(
        ids, gains, attn, attn_other, own_rows, wout, wout_other, cot, cot_other, *pieces_0
    )
    attn_all, cot_all, residual, normed_two, sum_mix, sum_norm = outs[:6]
    feed_0 = reduce_start(outs[6:])
    part, *grads_1 = call(
        feed_second_kernel,
        [SMEM] + [VMEM] * 4 + [VMEM] * 4,
        [(VMEM, shaped((2 * ROWS, WIDTH)))] + piece_shapes,
        weight_scratch,
        "feed_forward_and_back_second",
        20,
        2 * 10**10,
        10**8,
    )(ids, normed_two, cot_all, sum_mix, sum_norm, *pieces_1)
    part_other = swap(part, CORE)
    feed_0 = reduce_middle(*feed_0)
    feed_1 = reduce_start(grads_1)
    outs = call(
        backward_kernel,
        [SMEM] + [VMEM] * 11,
        [
            (VMEM, shaped((2, 64, WIDTH - 1))),
            (VMEM, shaped((2, 64, WIDTH), f32)),
            (VMEM, shaped((ROWS, HALF))),
            (VMEM, shaped((ROWS, HALF))),
            (VMEM, shaped((8, 2, 64, WIDTH))),
            (VMEM, shaped((8, 2, 64, WIDTH))),
            (VMEM, rows_shape),
        ],
        [
            pltpu.VMEM((ROWS, HALF), bf),
            pltpu.VMEM((2, POSITIONS, WIDTH), bf),
            pltpu.VMEM((ROWS, WIDTH), bf),
            pltpu.VMEM((ROWS, WIDTH), f32),
        ],
        "attention_backward",
        30,
    )(
        ids, gains, residual, part, part_other, cot_all, wout, wout_other, query,
        wqkv, kv, soft,
    )
    mixed, d_residual, *outs = outs
    outs, feed_0, feed_1 = fence(outs, feed_0, feed_1)
    d_query, d_sum_half, keep_rows, send_rows, d_kv = outs
    feed_0 = reduce_z(*feed_0)
    feed_1 = reduce_middle(*feed_1)
    got_rows = swap(send_rows, CORE)
    grad_attn_pieces = call(
        gradient_kernel,
        [SMEM] + [VMEM] * 5,
        [(VMEM, shaped((8, 48, 3 * HALF)))] * 2 + [(VMEM, shaped((8, 48, HALF)))] * 2,
        [
            pltpu.VMEM((WIDTH, 3 * HALF), bf),
            pltpu.VMEM((WIDTH, HALF), bf),
        ],
        "attention_weight_gradients",
        20,
    )(ids, attn_all, d_sum_half, d_query, d_kv, normed_all)
    keep_rows, got_rows, grad_attn_pieces, feed_1 = fence(
        keep_rows, got_rows, grad_attn_pieces, feed_1
    )
    crossed = swap(add(keep_rows[4:], got_rows[4:]).astype(bf), AXIS_X)
    attn_first = reduce_start(grad_attn_pieces)
    feed_1 = reduce_z(*feed_1)
    feed_1, crossed, attn_first = fence(feed_1, crossed, attn_first)
    rows_4 = add(keep_rows[:4], got_rows[:4], crossed).astype(bf)
    to_near = swap(rows_4[1], AXIS_Z_NEAR, downward(AXIS_Z_NEAR))
    to_far = swap(rows_4[2], AXIS_Z_FAR, downward(AXIS_Z_FAR))
    to_end = swap(rows_4[3], AXIS_Z_NEAR | AXIS_Z_FAR, downward(AXIS_Z_FAR))
    attn_last = reduce_z(*reduce_middle(*attn_first))
    sum_0, sum_1, attn_sum = add(*feed_0), add(*feed_1), add(*attn_last)
    (grad_tokens,) = call(
        tail_kernel,
        [VMEM] * 7,
        [(VMEM, shaped((2, 64, WIDTH - 1), f32))],
        [],
        "token_gradient",
        8,
        2 * 10**10,
        10**8,
    )(gains, own, rows_4[0], to_near, to_far, to_end, d_residual)
    attn_0, attn_1 = core_rows(core, attn_sum)
    up_sum = jnp.concatenate([sum_0[:, :WIDTH], sum_1[:, :WIDTH]], axis=-1)
    up_0, up_1 = core_rows(core, up_sum)
    grad_qkv = jnp.concatenate(
        [half[:, k * HALF : k * HALF + HALF] for k in range(3) for half in (attn_0, attn_1)],
        axis=-1,
    )
    grad_out = jnp.concatenate([attn_0[:, 3 * HALF :], attn_1[:, 3 * HALF : 4 * HALF - 1]], axis=-1)
    grad_up = join_units(up_0, up_1, 16)
    grad_down = jnp.concatenate([sum_0[:, WIDTH:], sum_1[:, WIDTH:]], axis=0)
    grad_gain_one = jnp.sum(grad_qkv * w_qkv.astype(f32), axis=-1) / gain_one.astype(f32)
    grad_gain_two = jnp.sum(grad_up * w_up.astype(f32), axis=-1) / gain_two.astype(f32)
    return (
        mixed[:, None],
        grad_tokens[:, None],
        grad_qkv,
        grad_out,
        grad_up,
        grad_down[:, : WIDTH - 1],
        grad_gain_one,
        grad_gain_two,
    )


def solution(mesh):
    small_slice = (mesh.shape["head"], mesh.shape["blk"]) == (2, 16)
    placed = (
        P(None, "head", "blk", None),
        P(None, "head", "blk"),
        P(None, "head", "blk", None),
        P(("head", "blk"), None),
        P(("head", "blk"), None),
        P(("head", "blk"), None),
        P(("head", "blk"), None),
        P(("head", "blk")),
        P(("head", "blk")),
    )
    return jax.shard_map(
        on_chip_pair if small_slice else on_device,
        mesh=mesh,
        in_specs=placed,
        out_specs=(
            P(None, "head", "blk", None),
            P(None, "head", "blk", None),
            P(("head", "blk"), None),
            P(("head", "blk"), None),
            P(("head", "blk"), None),
            P(("head", "blk"), None),
            P(("head", "blk")),
            P(("head", "blk")),
        ),
        check_vma=False,
    )
```

profile of v0, /device:TPU:0, one launch (start us, length us, event | category | flops | bytes accessed | tf_op | source)
XLA Modules:
  0.0 238.3 jit_solution(1759574229540425053)
XLA Ops:
  2.5 7.0 %collective-permute-start.2 = (bf16[2,64,768]{2,1,0:T(8,128)(2,1)S(1)}, bf16[2,64,768]{2,1,0:T(8,128)(2,1)S(1)}, u32[]{:S(2)}, u32[]{:S(2)}) collective-permute-start(bf16[2,64,768]{2,1,0:T(8,128)(2,1)S(1)} %get-tuple-element.203.tokens), channel_id=1, source_target_pairs={{0,12},{1,13},{2,14},{3,15},{4,8},{5,9},{6,10},{7,11},{16,28},{17,... | collective-permute-start | bytes 589832 | tf_op jit(solution)/shard_map/ppermute | solution.py:252
  9.5 1.3 collective-permute-start.1
  10.8 2.5 %collective-permute-start = (bf16[2,64,768]{2,1,0:T(8,128)(2,1)S(1)}, bf16[2,64,768]{2,1,0:T(8,128)(2,1)S(1)}, u32[]{:S(2)}, u32[]{:S(2)}) collective-permute-start(bf16[2,64,768]{2,1,0:T(8,128)(2,1)S(1)} %get-tuple-element.203.tokens), channel_id=1, source_target_pairs={{0,4},{1,5},{2,6},{3,7},{8,12},{9,13},{10,14},{11,15},{16,20},{17,... | collective-permute-start | bytes 589832 | tf_op jit(solution)/shard_map/ppermute | solution.py:252
  19.4 2.8 %collective-permute-done = bf16[2,64,768]{2,1,0:T(8,128)(2,1)S(1)} collective-permute-done((bf16[2,64,768]{2,1,0:T(8,128)(2,1)S(1)}, bf16[2,64,768]{2,1,0:T(8,128)(2,1)S(1)}, u32[]{:S(2)}, u32[]{:S(2)}) %collective-permute-start) | collective-permute-done | bytes 196640 | tf_op jit(solution)/shard_map/ppermute | solution.py:252
  22.2 1.6 collective-permute-start.3
  23.8 6.6 %collective-permute-start.8 = (bf16[48,1664]{1,0:T(8,128)(2,1)S(1)}, bf16[48,1664]{1,0:T(8,128)(2,1)S(1)}, u32[]{:S(2)}, u32[]{:S(2)}) collective-permute-start(bf16[48,1664]{1,0:T(8,128)(2,1)S(1)} %pad_maximum_fusion.9), channel_id=1, source_target_pairs={{0,12},{1,13},{2,14},{3,15},{4,8},{5,9},{6,10},{7,11},{8,4},{9,5},... | collective-permute-start | bytes 479240 | tf_op jit(solution)/shard_map/ppermute | solution.py:252
  31.1 4.3 %collective-permute-done.8 = bf16[48,1664]{1,0:T(8,128)(2,1)S(1)} collective-permute-done((bf16[48,1664]{1,0:T(8,128)(2,1)S(1)}, bf16[48,1664]{1,0:T(8,128)(2,1)S(1)}, u32[]{:S(2)}, u32[]{:S(2)}) %collective-permute-start.8) | collective-permute-done | bytes 159776 | tf_op jit(solution)/shard_map/ppermute | solution.py:252
  35.5 6.5 %collective-permute-done.7 = bf16[48,1664]{1,0:T(8,128)(2,1)S(1)} collective-permute-done((bf16[48,1664]{1,0:T(8,128)(2,1)S(1)}, bf16[48,1664]{1,0:T(8,128)(2,1)S(1)}, u32[]{:S(2)}, u32[]{:S(2)}) %collective-permute-start.7) | collective-permute-done | bytes 159776 | tf_op jit(solution)/shard_map/ppermute | solution.py:252
  42.1 5.3 %collective-permute-start.19 = (bf16[48,1536]{1,0:T(8,128)(2,1)S(1)}, bf16[48,1536]{1,0:T(8,128)(2,1)S(1)}, u32[]{:S(2)}, u32[]{:S(2)}) collective-permute-start(bf16[48,1536]{1,0:T(8,128)(2,1)S(1)} %pad_maximum_fusion.16), channel_id=1, source_target_pairs={{0,12},{1,13},{2,14},{3,15},{4,8},{5,9},{6,10},{7,11},{8,4},{9,5},... | collective-permute-start | bytes 442376 | tf_op jit(solution)/shard_map/ppermute | solution.py:252
  48.1 1.6 collective-permute-start.11
  49.7 1.6 collective-permute-start.9
  52.2 5.1 %collective-permute-done.18 = bf16[48,1536]{1,0:T(8,128)(2,1)S(1)} collective-permute-done((bf16[48,1536]{1,0:T(8,128)(2,1)S(1)}, bf16[48,1536]{1,0:T(8,128)(2,1)S(1)}, u32[]{:S(2)}, u32[]{:S(2)}) %collective-permute-start.18) | collective-permute-done | bytes 147488 | tf_op jit(solution)/shard_map/ppermute | solution.py:252
  57.3 2.6 %collective-permute-start.26 = (bf16[48,1536]{1,0:T(8,128)(2,1)S(1)}, bf16[48,1536]{1,0:T(8,128)(2,1)S(1)}, u32[]{:S(2)}, u32[]{:S(2)}) collective-permute-start(bf16[48,1536]{1,0:T(8,128)(2,1)S(1)} %fusion.26), channel_id=1, source_target_pairs={{0,12},{1,13},{2,14},{3,15},{4,8},{5,9},{6,10},{7,11},{8,4},{9,5},... | collective-permute-start | bytes 442376 | tf_op jit(solution)/shard_map/ppermute | solution.py:252
  60.0 1.7 collective-permute-start.24
  61.9 1.5 collective-permute-start.20
  63.5 1.6 collective-permute-start.22
  65.9 5.5 %collective-permute-done.25 = bf16[48,1536]{1,0:T(8,128)(2,1)S(1)} collective-permute-done((bf16[48,1536]{1,0:T(8,128)(2,1)S(1)}, bf16[48,1536]{1,0:T(8,128)(2,1)S(1)}, u32[]{:S(2)}, u32[]{:S(2)}) %collective-permute-start.25) | collective-permute-done | bytes 147488 | tf_op jit(solution)/shard_map/ppermute | solution.py:252
  71.4 1.5 collective-permute-start.12
  72.9 1.5 collective-permute-start.10
  75.9 5.4 %collective-permute-done.12.w3 = bf16[8,48,384]{2,1,0:T(8,128)(2,1)S(1)} collective-permute-done((bf16[8,48,384]{2,1,0:T(8,128)(2,1)S(1)}, bf16[8,48,384]{2,1,0:T(8,128)(2,1)S(1)}, u32[]{:S(2)}, u32[]{:S(2)}) %collective-permute-start.12) | collective-permute-done | bytes 294944 | tf_op jit(solution)/shard_map/ppermute | solution.py:252
  81.4 3.9 %collective-permute-done.27 = bf16[4,48,768]{2,1,0:T(8,128)(2,1)S(1)} collective-permute-done((bf16[4,48,768]{2,1,0:T(8,128)(2,1)S(1)}, bf16[4,48,768]{2,1,0:T(8,128)(2,1)S(1)}, u32[]{:S(2)}, u32[]{:S(2)}) %collective-permute-start.27) | collective-permute-done | bytes 294944 | tf_op jit(solution)/shard_map/ppermute | solution.py:252
  85.3 1.5 collective-permute-start.21
  86.8 10.7 %collective-permute-done.10.w1 = bf16[8,48,1280]{2,1,0:T(8,128)(2,1)S(1)} collective-permute-done((bf16[8,48,1280]{2,1,0:T(8,128)(2,1)S(1)}, bf16[8,48,1280]{2,1,0:T(8,128)(2,1)S(1)}, u32[]{:S(2)}, u32[]{:S(2)}) %collective-permute-start.10) | collective-permute-done | bytes 983072 | tf_op jit(solution)/shard_map/ppermute | solution.py:252
  98.1 1.5 collective-permute-start.28
  99.7 12.7 %attention_forward.1 = (bf16[256,384]{1,0:T(8,128)(2,1)S(1)}, bf16[256,384]{1,0:T(8,128)(2,1)S(1)}, bf16[256,768]{1,0:T(8,128)(2,1)S(1)}, f32[8,768]{1,0:T(8,128...) custom-call(s32[2]{0:T(128)S(1)} %pad_add_fusion.ids, ...), custom_call_target="tpu_custom_call" | custom-call | tf_op jit(solution)/shard_map/attention_forward/pallas_call | solution.py:714
  112.5 1.5 collective-permute-start.30
  114.0 2.6 %collective-permute-done.21.w1 = bf16[8,48,768]{2,1,0:T(8,128)(2,1)S(1)} collective-permute-done((bf16[8,48,768]{2,1,0:T(8,128)(2,1)S(1)}, bf16[8,48,768]{2,1,0:T(8,128)(2,1)S(1)}, u32[]{:S(2)}, u32[]{:S(2)}) %collective-permute-start.21) | collective-permute-done | bytes 589856 | tf_op jit(solution)/shard_map/ppermute | solution.py:252
  116.5 1.4 collective-permute-done.13.attn_other
  118.0 4.2 %feed_forward_and_back_first.1 = (bf16[256,768]{1,0:T(8,128)(2,1)S(1)}, bf16[256,768]{1,0:T(8,128)(2,1)S(1)}, f32[256,768]{1,0:T(8,128)S(1)}, bf16[256,768]{1,0:...) custom-call(s32[2]{0:T(128)S(1)} %pad_add_fusion.ids, ...), custom_call_target="tpu_custom_call" | custom-call | tf_op jit(solution)/shard_map/feed_forward_and_back_first/pallas_call | solution.py:740
  122.1 1.6 collective-permute-start.32
  124.3 3.6 %collective-permute-done.28.w1 = bf16[8,48,768]{2,1,0:T(8,128)(2,1)S(1)} collective-permute-done((bf16[8,48,768]{2,1,0:T(8,128)(2,1)S(1)}, bf16[8,48,768]{2,1,0:T(8,128)(2,1)S(1)}, u32[]{:S(2)}, u32[]{:S(2)}) %collective-permute-start.28) | collective-permute-done | bytes 589856 | tf_op jit(solution)/shard_map/ppermute | solution.py:252
  128.6 3.6 %feed_forward_and_back_second.1 = (bf16[512,768]{1,0:T(8,128)(2,1)S(1)}, bf16[8,48,768]{2,1,0:T(8,128)(2,1)S(1)}, bf16[8,48,768]{2,1,0:T(8,128)(2,1)S(1)}, bf16[...) custom-call(s32[2]{0:T(128)S(1)} %pad_add_fusion.ids, bf16[256,768]{1,0:T(8,128)(2,1)S(1)} %get-tuple-element.107.normed, ...), custom_call_target="tpu_custom_call" | custom-call | flops 20000000000 | bytes 100000000 | tf_op jit(solution)/shard_map/feed_forward_and_back_second/pallas_call | solution.py:760
  133.1 1.1 collective-permute-start.37
  134.3 6.3 %collective-permute-done.32 = bf16[8,48,768]{2,1,0:T(8,128)(2,1)S(1)} collective-permute-done((bf16[8,48,768]{2,1,0:T(8,128)(2,1)S(1)}, bf16[8,48,768]{2,1,0:T(8,128)(2,1)S(1)}, u32[]{:S(2)}, u32[]{:S(2)}) %collective-permute-start.32) | collective-permute-done | bytes 589856 | tf_op jit(solution)/shard_map/ppermute | solution.py:252
  141.4 1.6 collective-permute-start.35
  143.1 13.5 %attention_backward.1 = (bf16[2,64,767]{2,1,0:T(8,128)(2,1)}, f32[2,64,768]{2,1,0:T(8,128)S(1)}, bf16[256,384]{1,0:T(8,128)(2,1)S(1)}, bf16[256,384]{1,0:T(8,128...) custom-call(s32[2]{0:T(128)S(1)} %pad_add_fusion.ids, ...), custom_call_target="tpu_custom_call" | custom-call | tf_op jit(solution)/shard_map/attention_backward/pallas_call | solution.py:773
  156.6 3.2 %collective-permute-done.33 = bf16[4,48,768]{2,1,0:T(8,128)(2,1)S(1)} collective-permute-done((bf16[4,48,768]{2,1,0:T(8,128)(2,1)S(1)}, bf16[4,48,768]{2,1,0:T(8,128)(2,1)S(1)}, u32[]{:S(2)}, u32[]{:S(2)}) %collective-permute-start.33) | collective-permute-done | bytes 294944 | tf_op jit(solution)/shard_map/ppermute | solution.py:252
  160.6 1.5 collective-permute-start.39
  162.5 1.1 collective-permute-start.58
  163.6 4.3 %attention_weight_gradients.1 = (bf16[8,48,1152]{2,1,0:T(8,128)(2,1)S(1)}, bf16[8,48,1152]{2,1,0:T(8,128)(2,1)S(1)}, bf16[8,48,384]{2,1,0:T(8,128)(2,1)S(1)}, bf16[8,48,384]{2,1,0:T(8,128)(2,1)S(1)}) custom-call(s32[2]{0:T(128)S(1)} %pad_add_fusion.ids, bf16[256,768]{1,0:T(8,128)(2,1)S(1)} %get-tuple-element.137.attn, ...), custom_call_target="tpu_custom_call" | custom-call | tf_op jit(solution)/shard_map/attention_weight_gradients/pallas_call | solution.py:803
  167.9 1.5 collective-permute-done.40
  171.5 1.5 collective-permute-start.45
  173.3 1.1 collective-permute-start.43
  174.4 1.2 collective-permute-start.46
  175.6 7.4 %collective-permute-done.57 = bf16[48,1536]{1,0:T(8,128)(2,1)S(1)} collective-permute-done((bf16[48,1536]{1,0:T(8,128)(2,1)S(1)}, bf16[48,1536]{1,0:T(8,128)(2,1)S(1)}, u32[]{:S(2)}, u32[]{:S(2)}) %collective-permute-start.57) | collective-permute-done | bytes 147488 | tf_op jit(solution)/shard_map/ppermute | solution.py:252
  183.1 2.6 %collective-permute-start.42 = (bf16[48,1536]{1,0:T(8,128)(2,1)S(1)}, bf16[48,1536]{1,0:T(8,128)(2,1)S(1)}, u32[]{:S(2)}, u32[]{:S(2)}) collective-permute-start(bf16[48,1536]{1,0:T(8,128)(2,1)S(1)} %get-tuple-element.217), channel_id=1, source_target_pairs={{0,8},{1,9},{2,10},{3,11},{4,12},{5,13},{6,14},{7,15},{8,0},{9,1},... | collective-permute-start | bytes 442376 | tf_op jit(solution)/shard_map/ppermute | solution.py:252
  185.7 3.9 %collective-permute-done.41 = bf16[48,1536]{1,0:T(8,128)(2,1)S(1)} collective-permute-done((bf16[48,1536]{1,0:T(8,128)(2,1)S(1)}, bf16[48,1536]{1,0:T(8,128)(2,1)S(1)}, u32[]{:S(2)}, u32[]{:S(2)}) %collective-permute-start.41) | collective-permute-done | bytes 147488 | tf_op jit(solution)/shard_map/ppermute | solution.py:252
  189.6 3.1 %collective-permute-done.42 = bf16[48,1536]{1,0:T(8,128)(2,1)S(1)} collective-permute-done((bf16[48,1536]{1,0:T(8,128)(2,1)S(1)}, bf16[48,1536]{1,0:T(8,128)(2,1)S(1)}, u32[]{:S(2)}, u32[]{:S(2)}) %collective-permute-start.42) | collective-permute-done | bytes 147488 | tf_op jit(solution)/shard_map/ppermute | solution.py:252
  192.7 2.9 %collective-permute-done.46 = bf16[8,48,384]{2,1,0:T(8,128)(2,1)S(1)} collective-permute-done((bf16[8,48,384]{2,1,0:T(8,128)(2,1)S(1)}, bf16[8,48,384]{2,1,0:T(8,128)(2,1)S(1)}, u32[]{:S(2)}, u32[]{:S(2)}) %collective-permute-start.46) | collective-permute-done | bytes 294944 | tf_op jit(solution)/shard_map/ppermute | solution.py:252
  197.4 1.5 collective-permute-start.51
  198.9 1.3 collective-permute-start.49
  200.2 1.3 collective-permute-start.48
  202.6 1.2 collective-permute-start.50
  205.4 1.1 reshape.62
  206.5 1.2 multiply_reduce_fusion
  207.7 1.1 add_convert_fusion.12
  208.8 6.7 %collective-permute-done.50 = bf16[4,48,1152]{2,1,0:T(8,128)(2,1)} collective-permute-done((bf16[4,48,1152]{2,1,0:T(8,128)(2,1)}, bf16[4,48,1152]{2,1,0:T(8,128)(2,1)}, u32[]{:S(2)}, u32[]{:S(2)}) %collective-permute-start.50) | collective-permute-done | bytes 442400 | tf_op jit(solution)/shard_map/ppermute | solution.py:252
  215.5 1.3 add_convert_fusion.2
  216.9 1.3 collective-permute-start.52
  218.2 3.8 %collective-permute-start.54 = (bf16[48,1536]{1,0:T(8,128)(2,1)S(1)}, bf16[48,1536]{1,0:T(8,128)(2,1)S(1)}, u32[]{:S(2)}, u32[]{:S(2)}) collective-permute-start(bf16[48,1536]{1,0:T(8,128)(2,1)S(1)} %get-tuple-element.212), channel_id=1, source_target_pairs={{0,12},{1,13},{2,14},{3,15},{4,8},{5,9},{6,10},{7,11},{8,4},{9,5},... | collective-permute-start | bytes 442376 | tf_op jit(solution)/shard_map/ppermute | solution.py:252
  222.5 1.3 collective-permute-start.47
  223.8 6.1 %collective-permute-done.54 = bf16[48,1536]{1,0:T(8,128)(2,1)S(1)} collective-permute-done((bf16[48,1536]{1,0:T(8,128)(2,1)S(1)}, bf16[48,1536]{1,0:T(8,128)(2,1)S(1)}, u32[]{:S(2)}, u32[]{:S(2)}) %collective-permute-start.54) | collective-permute-done | bytes 147488 | tf_op jit(solution)/shard_map/ppermute | solution.py:252
  229.9 5.0 %collective-permute-done.53 = bf16[48,1536]{1,0:T(8,128)(2,1)S(1)} collective-permute-done((bf16[48,1536]{1,0:T(8,128)(2,1)S(1)}, bf16[48,1536]{1,0:T(8,128)(2,1)S(1)}, u32[]{:S(2)}, u32[]{:S(2)}) %collective-permute-start.53) | collective-permute-done | bytes 147488 | tf_op jit(solution)/shard_map/ppermute | solution.py:252
  235.3 1.2 token_gradient.1
  (229 shorter events, 27.3 us)
Async XLA Ops:
  0.6 14.6 %copy-start.13 = (bf16[24,767]{1,0:T(8,128)(2,1)S(1)}, bf16[24,767]{1,0:T(8,128)(2,1)}, u32[]{:S(2)}) copy-start(bf16[24,767]{1,0:T(8,128)(2,1)} %param.13) | copy-start | bytes 110452
  0.6 15.3 %copy-start.6 = (bf16[24,3072]{1,0:T(8,128)(2,1)S(1)}, bf16[24,3072]{1,0:T(8,128)(2,1)}, u32[]{:S(2)}) copy-start(bf16[24,3072]{1,0:T(8,128)(2,1)} %param.14) | copy-start | bytes 442372
  2.5 16.8 %collective-permute-start.2 = (bf16[2,64,768]{2,1,0:T(8,128)(2,1)S(1)}, bf16[2,64,768]{2,1,0:T(8,128)(2,1)S(1)}, u32[]{:S(2)}, u32[]{:S(2)}) collective-permute-start(bf16[2,64,768]{2,1,0:T(8,128)(2,1)S(1)} %get-tuple-element.203.tokens), channel_id=1, source_target_pairs={{0,12},{1,13},{2,14},{3,15},{4,8},{5,9},{6,10},{7,11},{16,28},{17,... | collective-permute-start | bytes 589832 | tf_op jit(solution)/shard_map/ppermute | solution.py:252
  9.5 9.9 %collective-permute-start.1 = (bf16[2,64,768]{2,1,0:T(8,128)(2,1)S(1)}, bf16[2,64,768]{2,1,0:T(8,128)(2,1)S(1)}, u32[]{:S(2)}, u32[]{:S(2)}) collective-permute-start(bf16[2,64,768]{2,1,0:T(8,128)(2,1)S(1)} %get-tuple-element.203.tokens), channel_id=1, source_target_pairs={{0,8},{1,9},{2,10},{3,11},{4,12},{5,13},{6,14},{7,15},{16,24},{17,... | collective-permute-start | bytes 589832 | tf_op jit(solution)/shard_map/ppermute | solution.py:252
  10.8 11.3 %collective-permute-start = (bf16[2,64,768]{2,1,0:T(8,128)(2,1)S(1)}, bf16[2,64,768]{2,1,0:T(8,128)(2,1)S(1)}, u32[]{:S(2)}, u32[]{:S(2)}) collective-permute-start(bf16[2,64,768]{2,1,0:T(8,128)(2,1)S(1)} %get-tuple-element.203.tokens), channel_id=1, source_target_pairs={{0,4},{1,5},{2,6},{3,7},{8,12},{9,13},{10,14},{11,15},{16,20},{17,... | collective-permute-start | bytes 589832 | tf_op jit(solution)/shard_map/ppermute | solution.py:252
  16.0 3.3 %collective-permute-start.5 = (bf16[24,1664]{1,0:T(8,128)(2,1)}, bf16[24,1664]{1,0:T(8,128)(2,1)S(1)}, u32[]{:S(2)}, u32[]{:S(2)}) collective-permute-start(bf16[24,1664]{1,0:T(8,128)(2,1)} %broadcast_select_fusion.2), channel_id=1, source_target_pairs={{0,1},{1,0},{2,3},{3,2},{4,5},{5,4},{6,7},{7,6},{8,9},{9,8},{10,11... | collective-permute-start | bytes 239624 | tf_op jit(solution)/shard_map/ppermute | solution.py:252
  17.6 1.6 collective-permute-start.16
  22.2 19.7 %collective-permute-start.3 = (bf16[4,2,64,768]{3,2,1,0:T(8,128)(2,1)S(1)}, bf16[4,2,64,768]{3,2,1,0:T(8,128)(2,1)S(1)}, u32[]{:S(2)}, u32[]{:S(2)}) collective-permute-start(bf16[4,2,64,768]{3,2,1,0:T(8,128)(2,1)S(1)} %pad_maximum_fusion), channel_id=1, source_target_pairs={{0,2},{1,3},{2,0},{3,1},{4,6},{5,7},{6,4},{7,5},{8,10},{9,11},{10,... | collective-permute-start | bytes 2359304 | tf_op jit(solution)/shard_map/ppermute | solution.py:252
  23.8 11.7 %collective-permute-start.8 = (bf16[48,1664]{1,0:T(8,128)(2,1)S(1)}, bf16[48,1664]{1,0:T(8,128)(2,1)S(1)}, u32[]{:S(2)}, u32[]{:S(2)}) collective-permute-start(bf16[48,1664]{1,0:T(8,128)(2,1)S(1)} %pad_maximum_fusion.9), channel_id=1, source_target_pairs={{0,12},{1,13},{2,14},{3,15},{4,8},{5,9},{6,10},{7,11},{8,4},{9,5},... | collective-permute-start | bytes 479240 | tf_op jit(solution)/shard_map/ppermute | solution.py:252
  30.4 11.5 %collective-permute-start.7 = (bf16[48,1664]{1,0:T(8,128)(2,1)S(1)}, bf16[48,1664]{1,0:T(8,128)(2,1)S(1)}, u32[]{:S(2)}, u32[]{:S(2)}) collective-permute-start(bf16[48,1664]{1,0:T(8,128)(2,1)S(1)} %pad_maximum_fusion.9), channel_id=1, source_target_pairs={{0,8},{1,9},{2,10},{3,11},{4,12},{5,13},{6,14},{7,15},{8,0},{9,1},... | collective-permute-start | bytes 479240 | tf_op jit(solution)/shard_map/ppermute | solution.py:252
  30.4 11.5 %collective-permute-start.6 = (bf16[48,1664]{1,0:T(8,128)(2,1)S(1)}, bf16[48,1664]{1,0:T(8,128)(2,1)S(1)}, u32[]{:S(2)}, u32[]{:S(2)}) collective-permute-start(bf16[48,1664]{1,0:T(8,128)(2,1)S(1)} %pad_maximum_fusion.9), channel_id=1, source_target_pairs={{0,4},{1,5},{2,6},{3,7},{4,0},{5,1},{6,2},{7,3},{8,12},{9,13},{10,... | collective-permute-start | bytes 479240 | tf_op jit(solution)/shard_map/ppermute | solution.py:252
  42.1 10.1 %collective-permute-start.19 = (bf16[48,1536]{1,0:T(8,128)(2,1)S(1)}, bf16[48,1536]{1,0:T(8,128)(2,1)S(1)}, u32[]{:S(2)}, u32[]{:S(2)}) collective-permute-start(bf16[48,1536]{1,0:T(8,128)(2,1)S(1)} %pad_maximum_fusion.16), channel_id=1, source_target_pairs={{0,12},{1,13},{2,14},{3,15},{4,8},{5,9},{6,10},{7,11},{8,4},{9,5},... | collective-permute-start | bytes 442376 | tf_op jit(solution)/shard_map/ppermute | solution.py:252
  47.4 10.0 %collective-permute-start.18 = (bf16[48,1536]{1,0:T(8,128)(2,1)S(1)}, bf16[48,1536]{1,0:T(8,128)(2,1)S(1)}, u32[]{:S(2)}, u32[]{:S(2)}) collective-permute-start(bf16[48,1536]{1,0:T(8,128)(2,1)S(1)} %pad_maximum_fusion.16), channel_id=1, source_target_pairs={{0,8},{1,9},{2,10},{3,11},{4,12},{5,13},{6,14},{7,15},{8,0},{9,1},... | collective-permute-start | bytes 442376 | tf_op jit(solution)/shard_map/ppermute | solution.py:252
  47.4 10.0 %collective-permute-start.17 = (bf16[48,1536]{1,0:T(8,128)(2,1)S(1)}, bf16[48,1536]{1,0:T(8,128)(2,1)S(1)}, u32[]{:S(2)}, u32[]{:S(2)}) collective-permute-start(bf16[48,1536]{1,0:T(8,128)(2,1)S(1)} %pad_maximum_fusion.16), channel_id=1, source_target_pairs={{0,4},{1,5},{2,6},{3,7},{4,0},{5,1},{6,2},{7,3},{8,12},{9,13},{10,... | collective-permute-start | bytes 442376 | tf_op jit(solution)/shard_map/ppermute | solution.py:252
  48.1 13.7 %collective-permute-start.11 = (bf16[4,48,384]{2,1,0:T(8,128)(2,1)S(1)}, bf16[4,48,384]{2,1,0:T(8,128)(2,1)S(1)}, u32[]{:S(2)}, u32[]{:S(2)}) collective-permute-start(bf16[4,48,384]{2,1,0:T(8,128)(2,1)S(1)} %pad_maximum_fusion.15), channel_id=1, source_target_pairs={{0,16},{1,17},{2,18},{3,19},{4,20},{5,21},{6,22},{7,23},{8,24},{9,... | collective-permute-start | bytes 442376 | tf_op jit(solution)/shard_map/ppermute | solution.py:252
  49.7 12.0 %collective-permute-start.9 = (bf16[4,48,1280]{2,1,0:T(8,128)(2,1)S(1)}, bf16[4,48,1280]{2,1,0:T(8,128)(2,1)S(1)}, u32[]{:S(2)}, u32[]{:S(2)}) collective-permute-start(bf16[4,48,1280]{2,1,0:T(8,128)(2,1)S(1)} %pad_maximum_fusion.2), channel_id=1, source_target_pairs={{0,2},{1,3},{2,0},{3,1},{4,6},{5,7},{6,4},{7,5},{8,10},{9,11},{10,... | collective-permute-start | bytes 1474568 | tf_op jit(solution)/shard_map/ppermute | solution.py:252
  57.3 8.6 %collective-permute-start.26 = (bf16[48,1536]{1,0:T(8,128)(2,1)S(1)}, bf16[48,1536]{1,0:T(8,128)(2,1)S(1)}, u32[]{:S(2)}, u32[]{:S(2)}) collective-permute-start(bf16[48,1536]{1,0:T(8,128)(2,1)S(1)} %fusion.26), channel_id=1, source_target_pairs={{0,12},{1,13},{2,14},{3,15},{4,8},{5,9},{6,10},{7,11},{8,4},{9,5},... | collective-permute-start | bytes 442376 | tf_op jit(solution)/shard_map/ppermute | solution.py:252
  60.0 11.4 %collective-permute-start.25 = (bf16[48,1536]{1,0:T(8,128)(2,1)S(1)}, bf16[48,1536]{1,0:T(8,128)(2,1)S(1)}, u32[]{:S(2)}, u32[]{:S(2)}) collective-permute-start(bf16[48,1536]{1,0:T(8,128)(2,1)S(1)} %fusion.26), channel_id=1, source_target_pairs={{0,8},{1,9},{2,10},{3,11},{4,12},{5,13},{6,14},{7,15},{8,0},{9,1},... | collective-permute-start | bytes 442376 | tf_op jit(solution)/shard_map/ppermute | solution.py:252
  60.0 12.9 %collective-permute-start.24 = (bf16[48,1536]{1,0:T(8,128)(2,1)S(1)}, bf16[48,1536]{1,0:T(8,128)(2,1)S(1)}, u32[]{:S(2)}, u32[]{:S(2)}) collective-permute-start(bf16[48,1536]{1,0:T(8,128)(2,1)S(1)} %fusion.26), channel_id=1, source_target_pairs={{0,4},{1,5},{2,6},{3,7},{4,0},{5,1},{6,2},{7,3},{8,12},{9,13},{10,... | collective-permute-start | bytes 442376 | tf_op jit(solution)/shard_map/ppermute | solution.py:252
  61.9 12.5 %collective-permute-start.20 = (bf16[4,48,768]{2,1,0:T(8,128)(2,1)S(1)}, bf16[4,48,768]{2,1,0:T(8,128)(2,1)S(1)}, u32[]{:S(2)}, u32[]{:S(2)}) collective-permute-start(bf16[4,48,768]{2,1,0:T(8,128)(2,1)S(1)} %pad_maximum_fusion.4), channel_id=1, source_target_pairs={{0,2},{1,3},{2,0},{3,1},{4,6},{5,7},{6,4},{7,5},{8,10},{9,11},{10,... | collective-permute-start | bytes 884744 | tf_op jit(solution)/shard_map/ppermute | solution.py:252
  63.5 10.9 %collective-permute-start.22 = (bf16[4,48,768]{2,1,0:T(8,128)(2,1)S(1)}, bf16[4,48,768]{2,1,0:T(8,128)(2,1)S(1)}, u32[]{:S(2)}, u32[]{:S(2)}) collective-permute-start(bf16[4,48,768]{2,1,0:T(8,128)(2,1)S(1)} %pad_maximum_fusion.5), channel_id=1, source_target_pairs={{0,16},{1,17},{2,18},{3,19},{4,20},{5,21},{6,22},{7,23},{8,24},{9,... | collective-permute-start | bytes 884744 | tf_op jit(solution)/shard_map/ppermute | solution.py:252
  65.9 32.2 %collective-permute-start.4 = (bf16[8,2,64,768]{3,2,1,0:T(8,128)(2,1)S(1)}, bf16[8,2,64,768]{3,2,1,0:T(8,128)(2,1)S(1)}, u32[]{:S(2)}, u32[]{:S(2)}) collective-permute-start(bf16[8,2,64,768]{3,2,1,0:T(8,128)(2,1)S(1)} %constant_dynamic-update-slice_fusion.tok_mine), channel_id=1, source_target_pairs={{0,1},{1,0},{2,3},{3,2},{4,5},{5,4},{6,7},{7,6},{8,9},{9,8},{10,11... | collective-permute-start | bytes 4718600 | tf_op jit(solution)/shard_map/ppermute | solution.py:252
  71.4 9.9 %collective-permute-start.12 = (bf16[8,48,384]{2,1,0:T(8,128)(2,1)S(1)}, bf16[8,48,384]{2,1,0:T(8,128)(2,1)S(1)}, u32[]{:S(2)}, u32[]{:S(2)}) collective-permute-start(bf16[8,48,384]{2,1,0:T(8,128)(2,1)S(1)} %constant_dynamic-update-slice_fusion.20.w2), channel_id=1, source_target_pairs={{0,2},{1,3},{2,0},{3,1},{4,6},{5,7},{6,4},{7,5},{8,10},{9,11},{10,... | collective-permute-start | bytes 884744 | tf_op jit(solution)/shard_map/ppermute | solution.py:252
  72.9 24.7 %collective-permute-start.10 = (bf16[8,48,1280]{2,1,0:T(8,128)(2,1)S(1)}, bf16[8,48,1280]{2,1,0:T(8,128)(2,1)S(1)}, u32[]{:S(2)}, u32[]{:S(2)}) collective-permute-start(bf16[8,48,1280]{2,1,0:T(8,128)(2,1)S(1)} %constant_dynamic-update-slice_fusion.15.w0), channel_id=1, source_target_pairs={{0,16},{1,17},{2,18},{3,19},{4,20},{5,21},{6,22},{7,23},{8,24},{9,... | collective-permute-start | bytes 2949128 | tf_op jit(solution)/shard_map/ppermute | solution.py:252
  74.5 10.8 %collective-permute-start.27 = (bf16[4,48,768]{2,1,0:T(8,128)(2,1)S(1)}, bf16[4,48,768]{2,1,0:T(8,128)(2,1)S(1)}, u32[]{:S(2)}, u32[]{:S(2)}) collective-permute-start(bf16[4,48,768]{2,1,0:T(8,128)(2,1)S(1)} %pad_maximum_fusion.6), channel_id=1, source_target_pairs={{0,2},{1,3},{2,0},{3,1},{4,6},{5,7},{6,4},{7,5},{8,10},{9,11},{10,... | collective-permute-start | bytes 884744 | tf_op jit(solution)/shard_map/ppermute | solution.py:252
  75.2 37.1 %collective-permute-start.29 = (bf16[4,48,768]{2,1,0:T(8,128)(2,1)S(1)}, bf16[4,48,768]{2,1,0:T(8,128)(2,1)S(1)}, u32[]{:S(2)}, u32[]{:S(2)}) collective-permute-start(bf16[4,48,768]{2,1,0:T(8,128)(2,1)S(1)} %pad_maximum_fusion.7), channel_id=1, source_target_pairs={{0,16},{1,17},{2,18},{3,19},{4,20},{5,21},{6,22},{7,23},{8,24},{9,... | collective-permute-start | bytes 884744 | tf_op jit(solution)/shard_map/ppermute | solution.py:252
  81.4 31.1 %collective-permute-start.15 = (bf16[2,64,768]{2,1,0:T(8,128)(2,1)S(1)}, bf16[2,64,768]{2,1,0:T(8,128)(2,1)S(1)}, u32[]{:S(2)}, u32[]{:S(2)}) collective-permute-start(bf16[2,64,768]{2,1,0:T(8,128)(2,1)S(1)} %pad.18.cot_mine), channel_id=1, source_target_pairs={{0,1},{1,0},{2,3},{3,2},{4,5},{5,4},{6,7},{7,6},{8,9},{9,8},{10,11... | collective-permute-start | bytes 589832 | tf_op jit(solution)/shard_map/ppermute | solution.py:252
  85.3 31.2 %collective-permute-start.21 = (bf16[8,48,768]{2,1,0:T(8,128)(2,1)S(1)}, bf16[8,48,768]{2,1,0:T(8,128)(2,1)S(1)}, u32[]{:S(2)}, u32[]{:S(2)}) collective-permute-start(bf16[8,48,768]{2,1,0:T(8,128)(2,1)S(1)} %constant_dynamic-update-slice_fusion.25.w0), channel_id=1, source_target_pairs={{0,16},{1,17},{2,18},{3,19},{4,20},{5,21},{6,22},{7,23},{8,24},{9,... | collective-permute-start | bytes 1769480 | tf_op jit(solution)/shard_map/ppermute | solution.py:252
  97.6 19.0 %collective-permute-start.23 = (bf16[8,48,768]{2,1,0:T(8,128)(2,1)S(1)}, bf16[8,48,768]{2,1,0:T(8,128)(2,1)S(1)}, u32[]{:S(2)}, u32[]{:S(2)}) collective-permute-start(bf16[8,48,768]{2,1,0:T(8,128)(2,1)S(1)} %constant_dynamic-update-slice_fusion.30.w2), channel_id=1, source_target_pairs={{0,2},{1,3},{2,0},{3,1},{4,6},{5,7},{6,4},{7,5},{8,10},{9,11},{10,... | collective-permute-start | bytes 1769480 | tf_op jit(solution)/shard_map/ppermute | solution.py:252
  98.1 29.8 %collective-permute-start.28 = (bf16[8,48,768]{2,1,0:T(8,128)(2,1)S(1)}, bf16[8,48,768]{2,1,0:T(8,128)(2,1)S(1)}, u32[]{:S(2)}, u32[]{:S(2)}) collective-permute-start(bf16[8,48,768]{2,1,0:T(8,128)(2,1)S(1)} %constant_dynamic-update-slice_fusion.35.w0), channel_id=1, source_target_pairs={{0,16},{1,17},{2,18},{3,19},{4,20},{5,21},{6,22},{7,23},{8,24},{9,... | collective-permute-start | bytes 1769480 | tf_op jit(solution)/shard_map/ppermute | solution.py:252
  112.3 5.6 %collective-permute-start.14 = (bf16[768,384]{1,0:T(8,128)(2,1)S(1)}, bf16[768,384]{1,0:T(8,128)(2,1)S(1)}, u32[]{:S(2)}, u32[]{:S(2)}) collective-permute-start(bf16[768,384]{1,0:T(8,128)(2,1)S(1)} %get-tuple-element.100.wout_mine), channel_id=1, source_target_pairs={{0,1},{1,0},{2,3},{3,2},{4,5},{5,4},{6,7},{7,6},{8,9},{9,8},{10,11... | collective-permute-start | bytes 1769480 | tf_op jit(solution)/shard_map/ppermute | solution.py:252
  112.5 16.2 %collective-permute-start.30 = (bf16[8,48,768]{2,1,0:T(8,128)(2,1)S(1)}, bf16[8,48,768]{2,1,0:T(8,128)(2,1)S(1)}, u32[]{:S(2)}, u32[]{:S(2)}) collective-permute-start(bf16[8,48,768]{2,1,0:T(8,128)(2,1)S(1)} %constant_dynamic-update-slice_fusion.40.w2), channel_id=1, source_target_pairs={{0,2},{1,3},{2,0},{3,1},{4,6},{5,7},{6,4},{7,5},{8,10},{9,11},{10,... | collective-permute-start | bytes 1769480 | tf_op jit(solution)/shard_map/ppermute | solution.py:252
  116.5 1.4 collective-permute-start.13
  122.1 18.4 %collective-permute-start.32 = (bf16[8,48,768]{2,1,0:T(8,128)(2,1)S(1)}, bf16[8,48,768]{2,1,0:T(8,128)(2,1)S(1)}, u32[]{:S(2)}, u32[]{:S(2)}) collective-permute-start(bf16[8,48,768]{2,1,0:T(8,128)(2,1)S(1)} %get-tuple-element.128), channel_id=1, source_target_pairs={{0,16},{1,17},{2,18},{3,19},{4,20},{5,21},{6,22},{7,23},{8,24},{9,... | collective-permute-start | bytes 1769480 | tf_op jit(solution)/shard_map/ppermute | solution.py:252
  123.7 17.6 %collective-permute-start.34 = (bf16[8,48,768]{2,1,0:T(8,128)(2,1)S(1)}, bf16[8,48,768]{2,1,0:T(8,128)(2,1)S(1)}, u32[]{:S(2)}, u32[]{:S(2)}) collective-permute-start(bf16[8,48,768]{2,1,0:T(8,128)(2,1)S(1)} %get-tuple-element.130), channel_id=1, source_target_pairs={{0,2},{1,3},{2,0},{3,1},{4,6},{5,7},{6,4},{7,5},{8,10},{9,11},{10,... | collective-permute-start | bytes 1769480 | tf_op jit(solution)/shard_map/ppermute | solution.py:252
  132.2 24.3 %collective-permute-start.36 = (bf16[8,48,768]{2,1,0:T(8,128)(2,1)S(1)}, bf16[8,48,768]{2,1,0:T(8,128)(2,1)S(1)}, u32[]{:S(2)}, u32[]{:S(2)}) collective-permute-start(bf16[8,48,768]{2,1,0:T(8,128)(2,1)S(1)} %get-tuple-element.132), channel_id=1, source_target_pairs={{0,16},{1,17},{2,18},{3,19},{4,20},{5,21},{6,22},{7,23},{8,24},{9,... | collective-permute-start | bytes 1769480 | tf_op jit(solution)/shard_map/ppermute | solution.py:252
  133.1 23.5 %collective-permute-start.37 = (bf16[8,48,768]{2,1,0:T(8,128)(2,1)S(1)}, bf16[8,48,768]{2,1,0:T(8,128)(2,1)S(1)}, u32[]{:S(2)}, u32[]{:S(2)}) collective-permute-start(bf16[8,48,768]{2,1,0:T(8,128)(2,1)S(1)} %get-tuple-element.134), channel_id=1, source_target_pairs={{0,2},{1,3},{2,0},{3,1},{4,6},{5,7},{6,4},{7,5},{8,10},{9,11},{10,... | collective-permute-start | bytes 1769480 | tf_op jit(solution)/shard_map/ppermute | solution.py:252
  134.3 8.8 %collective-permute-start.31 = (bf16[512,768]{1,0:T(8,128)(2,1)S(1)}, bf16[512,768]{1,0:T(8,128)(2,1)S(1)}, u32[]{:S(2)}, u32[]{:S(2)}) collective-permute-start(bf16[512,768]{1,0:T(8,128)(2,1)S(1)} %get-tuple-element.116.part_mine), channel_id=1, source_target_pairs={{0,1},{1,0},{2,3},{3,2},{4,5},{5,4},{6,7},{7,6},{8,9},{9,8},{10,11... | collective-permute-start | bytes 2359304 | tf_op jit(solution)/shard_map/ppermute | solution.py:252
  140.6 19.2 %collective-permute-start.33 = (bf16[4,48,768]{2,1,0:T(8,128)(2,1)S(1)}, bf16[4,48,768]{2,1,0:T(8,128)(2,1)S(1)}, u32[]{:S(2)}, u32[]{:S(2)}) collective-permute-start(bf16[4,48,768]{2,1,0:T(8,128)(2,1)S(1)} %add_convert_fusion.11), channel_id=1, source_target_pairs={{0,2},{1,3},{2,0},{3,1},{4,6},{5,7},{6,4},{7,5},{8,10},{9,11},{10,... | collective-permute-start | bytes 884744 | tf_op jit(solution)/shard_map/ppermute | solution.py:252
  141.4 18.4 %collective-permute-start.35 = (bf16[4,48,768]{2,1,0:T(8,128)(2,1)S(1)}, bf16[4,48,768]{2,1,0:T(8,128)(2,1)S(1)}, u32[]{:S(2)}, u32[]{:S(2)}) collective-permute-start(bf16[4,48,768]{2,1,0:T(8,128)(2,1)S(1)} %add_convert_fusion.10), channel_id=1, source_target_pairs={{0,16},{1,17},{2,18},{3,19},{4,20},{5,21},{6,22},{7,23},{8,24},{9,... | collective-permute-start | bytes 884744 | tf_op jit(solution)/shard_map/ppermute | solution.py:252
  159.8 10.5 %collective-permute-start.38 = (bf16[8,2,64,768]{3,2,1,0:T(8,128)(2,1)S(1)}, bf16[8,2,64,768]{3,2,1,0:T(8,128)(2,1)S(1)}, u32[]{:S(2)}, u32[]{:S(2)}) collective-permute-start(bf16[8,2,64,768]{3,2,1,0:T(8,128)(2,1)S(1)} %get-tuple-element.136), channel_id=1, source_target_pairs={{0,1},{1,0},{2,3},{3,2},{4,5},{5,4},{6,7},{7,6},{8,9},{9,8},{10,11... | collective-permute-start | bytes 4718600 | tf_op jit(solution)/shard_map/ppermute | solution.py:252
  159.9 9.5 %collective-permute-start.40 = (bf16[4,48,768]{2,1,0:T(8,128)(2,1)S(1)}, bf16[4,48,768]{2,1,0:T(8,128)(2,1)S(1)}, u32[]{:S(2)}, u32[]{:S(2)}) collective-permute-start(bf16[4,48,768]{2,1,0:T(8,128)(2,1)S(1)} %add_convert_fusion.8), channel_id=1, source_target_pairs={{0,16},{1,17},{2,18},{3,19},{4,20},{5,21},{6,22},{7,23},{8,24},{9,... | collective-permute-start | bytes 884744 | tf_op jit(solution)/shard_map/ppermute | solution.py:252
  160.6 9.8 %collective-permute-start.39 = (bf16[4,48,768]{2,1,0:T(8,128)(2,1)S(1)}, bf16[4,48,768]{2,1,0:T(8,128)(2,1)S(1)}, u32[]{:S(2)}, u32[]{:S(2)}) collective-permute-start(bf16[4,48,768]{2,1,0:T(8,128)(2,1)S(1)} %add_convert_fusion.9), channel_id=1, source_target_pairs={{0,2},{1,3},{2,0},{3,1},{4,6},{5,7},{6,4},{7,5},{8,10},{9,11},{10,... | collective-permute-start | bytes 884744 | tf_op jit(solution)/shard_map/ppermute | solution.py:252
  162.5 10.9 %collective-permute-start.56 = (bf16[48,1536]{1,0:T(8,128)(2,1)S(1)}, bf16[48,1536]{1,0:T(8,128)(2,1)S(1)}, u32[]{:S(2)}, u32[]{:S(2)}) collective-permute-start(bf16[48,1536]{1,0:T(8,128)(2,1)S(1)} %get-tuple-element.208), channel_id=1, source_target_pairs={{0,4},{1,5},{2,6},{3,7},{4,0},{5,1},{6,2},{7,3},{8,12},{9,13},{10,... | collective-permute-start | bytes 442376 | tf_op jit(solution)/shard_map/ppermute | solution.py:252
  162.5 11.9 %collective-permute-start.58 = (bf16[48,1536]{1,0:T(8,128)(2,1)S(1)}, bf16[48,1536]{1,0:T(8,128)(2,1)S(1)}, u32[]{:S(2)}, u32[]{:S(2)}) collective-permute-start(bf16[48,1536]{1,0:T(8,128)(2,1)S(1)} %get-tuple-element.209), channel_id=1, source_target_pairs={{0,12},{1,13},{2,14},{3,15},{4,8},{5,9},{6,10},{7,11},{8,4},{9,5},... | collective-permute-start | bytes 442376 | tf_op jit(solution)/shard_map/ppermute | solution.py:252
  169.4 13.5 %collective-permute-start.57 = (bf16[48,1536]{1,0:T(8,128)(2,1)S(1)}, bf16[48,1536]{1,0:T(8,128)(2,1)S(1)}, u32[]{:S(2)}, u32[]{:S(2)}) collective-permute-start(bf16[48,1536]{1,0:T(8,128)(2,1)S(1)} %get-tuple-element.210), channel_id=1, source_target_pairs={{0,8},{1,9},{2,10},{3,11},{4,12},{5,13},{6,14},{7,15},{8,0},{9,1},... | collective-permute-start | bytes 442376 | tf_op jit(solution)/shard_map/ppermute | solution.py:252
  170.6 24.9 %collective-permute-start.44 = (bf16[4,2,64,768]{3,2,1,0:T(8,128)(2,1)S(1)}, bf16[4,2,64,768]{3,2,1,0:T(8,128)(2,1)S(1)}, u32[]{:S(2)}, u32[]{:S(2)}) collective-permute-start(bf16[4,2,64,768]{3,2,1,0:T(8,128)(2,1)S(1)} %add_convert_fusion.1), channel_id=1, source_target_pairs={{0,2},{1,3},{2,0},{3,1},{4,6},{5,7},{6,4},{7,5},{8,10},{9,11},{10,... | collective-permute-start | bytes 2359304 | tf_op jit(solution)/shard_map/ppermute | solution.py:252
  171.5 24.0 %collective-permute-start.45 = (bf16[8,48,1152]{2,1,0:T(8,128)(2,1)S(1)}, bf16[8,48,1152]{2,1,0:T(8,128)(2,1)S(1)}, u32[]{:S(2)}, u32[]{:S(2)}) collective-permute-start(bf16[8,48,1152]{2,1,0:T(8,128)(2,1)S(1)} %get-tuple-element.159), channel_id=1, source_target_pairs={{0,16},{1,17},{2,18},{3,19},{4,20},{5,21},{6,22},{7,23},{8,24},{9,... | collective-permute-start | bytes 2654216 | tf_op jit(solution)/shard_map/ppermute | solution.py:252
  173.3 9.8 %collective-permute-start.43 = (bf16[48,1536]{1,0:T(8,128)(2,1)S(1)}, bf16[48,1536]{1,0:T(8,128)(2,1)S(1)}, u32[]{:S(2)}, u32[]{:S(2)}) collective-permute-start(bf16[48,1536]{1,0:T(8,128)(2,1)S(1)} %get-tuple-element.214), channel_id=1, source_target_pairs={{0,12},{1,13},{2,14},{3,15},{4,8},{5,9},{6,10},{7,11},{8,4},{9,5},... | collective-permute-start | bytes 442376 | tf_op jit(solution)/shard_map/ppermute | solution.py:252
  174.4 21.1 %collective-permute-start.46 = (bf16[8,48,384]{2,1,0:T(8,128)(2,1)S(1)}, bf16[8,48,384]{2,1,0:T(8,128)(2,1)S(1)}, u32[]{:S(2)}, u32[]{:S(2)}) collective-permute-start(bf16[8,48,384]{2,1,0:T(8,128)(2,1)S(1)} %get-tuple-element.161), channel_id=1, source_target_pairs={{0,2},{1,3},{2,0},{3,1},{4,6},{5,7},{6,4},{7,5},{8,10},{9,11},{10,... | collective-permute-start | bytes 884744 | tf_op jit(solution)/shard_map/ppermute | solution.py:252
  183.0 6.6 %collective-permute-start.41 = (bf16[48,1536]{1,0:T(8,128)(2,1)S(1)}, bf16[48,1536]{1,0:T(8,128)(2,1)S(1)}, u32[]{:S(2)}, u32[]{:S(2)}) collective-permute-start(bf16[48,1536]{1,0:T(8,128)(2,1)S(1)} %get-tuple-element.216), channel_id=1, source_target_pairs={{0,4},{1,5},{2,6},{3,7},{4,0},{5,1},{6,2},{7,3},{8,12},{9,13},{10,... | collective-permute-start | bytes 442376 | tf_op jit(solution)/shard_map/ppermute | solution.py:252
  183.1 9.6 %collective-permute-start.42 = (bf16[48,1536]{1,0:T(8,128)(2,1)S(1)}, bf16[48,1536]{1,0:T(8,128)(2,1)S(1)}, u32[]{:S(2)}, u32[]{:S(2)}) collective-permute-start(bf16[48,1536]{1,0:T(8,128)(2,1)S(1)} %get-tuple-element.217), channel_id=1, source_target_pairs={{0,8},{1,9},{2,10},{3,11},{4,12},{5,13},{6,14},{7,15},{8,0},{9,1},... | collective-permute-start | bytes 442376 | tf_op jit(solution)/shard_map/ppermute | solution.py:252
  197.4 10.3 %collective-permute-start.51 = (bf16[4,48,384]{2,1,0:T(8,128)(2,1)}, bf16[4,48,384]{2,1,0:T(8,128)(2,1)}, u32[]{:S(2)}, u32[]{:S(2)}) collective-permute-start(bf16[4,48,384]{2,1,0:T(8,128)(2,1)} %add_convert_fusion.13), channel_id=1, source_target_pairs={{0,16},{1,17},{2,18},{3,19},{4,20},{5,21},{6,22},{7,23},{8,24},{9,... | collective-permute-start | bytes 442376 | tf_op jit(solution)/shard_map/ppermute | solution.py:252
  198.9 36.2 %collective-permute-start.49 = (bf16[2,64,768]{2,1,0:T(8,128)(2,1)}, bf16[2,64,768]{2,1,0:T(8,128)(2,1)S(1)}, u32[]{:S(2)}, u32[]{:S(2)}) collective-permute-start(bf16[2,64,768]{2,1,0:T(8,128)(2,1)} %get-tuple-element.204), channel_id=1, source_target_pairs={{8,4},{9,5},{10,6},{11,7},{12,0},{13,1},{14,2},{15,3},{24,20},{25,... | collective-permute-start | bytes 589832 | tf_op jit(solution)/shard_map/ppermute | solution.py:252
  200.2 35.0 %collective-permute-start.48 = (bf16[2,64,768]{2,1,0:T(8,128)(2,1)}, bf16[2,64,768]{2,1,0:T(8,128)(2,1)S(1)}, u32[]{:S(2)}, u32[]{:S(2)}) collective-permute-start(bf16[2,64,768]{2,1,0:T(8,128)(2,1)} %get-tuple-element.205), channel_id=1, source_target_pairs={{8,0},{9,1},{10,2},{11,3},{12,4},{13,5},{14,6},{15,7},{24,16},{25,... | collective-permute-start | bytes 589832 | tf_op jit(solution)/shard_map/ppermute | solution.py:252
  201.7 2.9 %collective-permute-start.59 = (f32[24,1536]{1,0:T(8,128)S(1)}, f32[24,1536]{1,0:T(8,128)S(1)}, u32[]{:S(2)}, u32[]{:S(2)}) collective-permute-start(f32[24,1536]{1,0:T(8,128)S(1)} %broadcast_select_fusion.6), channel_id=1, source_target_pairs={{0,1},{1,0},{2,3},{3,2},{4,5},{5,4},{6,7},{7,6},{8,9},{9,8},{10,11... | collective-permute-start | bytes 442376 | tf_op jit(solution)/shard_map/ppermute | solution.py:252
  202.6 12.9 %collective-permute-start.50 = (bf16[4,48,1152]{2,1,0:T(8,128)(2,1)}, bf16[4,48,1152]{2,1,0:T(8,128)(2,1)}, u32[]{:S(2)}, u32[]{:S(2)}) collective-permute-start(bf16[4,48,1152]{2,1,0:T(8,128)(2,1)} %add_convert_fusion.3), channel_id=1, source_target_pairs={{0,2},{1,3},{2,0},{3,1},{4,6},{5,7},{6,4},{7,5},{8,10},{9,11},{10,... | collective-permute-start | bytes 1327112 | tf_op jit(solution)/shard_map/ppermute | solution.py:252
  207.7 14.3 %copy-start.14 = (bf16[24]{0:T(256)(128)(2,1)S(1)}, bf16[24]{0:T(256)(128)(2,1)}, u32[]{:S(2)}) copy-start(bf16[24]{0:T(256)(128)(2,1)} %param.17) | copy-start | bytes 148
  207.7 14.8 %copy-start.10 = (bf16[2,64,768]{2,1,0:T(8,128)(2,1)S(1)}, bf16[2,64,768]{2,1,0:T(8,128)(2,1)}, u32[]{:S(2)}) copy-start(bf16[2,64,768]{2,1,0:T(8,128)(2,1)} %get-tuple-element.206) | copy-start | bytes 589828
  216.9 5.6 %collective-permute-start.52 = (bf16[48,1536]{1,0:T(8,128)(2,1)S(1)}, bf16[48,1536]{1,0:T(8,128)(2,1)S(1)}, u32[]{:S(2)}, u32[]{:S(2)}) collective-permute-start(bf16[48,1536]{1,0:T(8,128)(2,1)S(1)} %get-tuple-element.211), channel_id=1, source_target_pairs={{0,4},{1,5},{2,6},{3,7},{4,0},{5,1},{6,2},{7,3},{8,12},{9,13},{10,... | collective-permute-start | bytes 442376 | tf_op jit(solution)/shard_map/ppermute | solution.py:252
  218.2 11.7 %collective-permute-start.54 = (bf16[48,1536]{1,0:T(8,128)(2,1)S(1)}, bf16[48,1536]{1,0:T(8,128)(2,1)S(1)}, u32[]{:S(2)}, u32[]{:S(2)}) collective-permute-start(bf16[48,1536]{1,0:T(8,128)(2,1)S(1)} %get-tuple-element.212), channel_id=1, source_target_pairs={{0,12},{1,13},{2,14},{3,15},{4,8},{5,9},{6,10},{7,11},{8,4},{9,5},... | collective-permute-start | bytes 442376 | tf_op jit(solution)/shard_map/ppermute | solution.py:252
  222.0 13.0 %collective-permute-start.53 = (bf16[48,1536]{1,0:T(8,128)(2,1)S(1)}, bf16[48,1536]{1,0:T(8,128)(2,1)S(1)}, u32[]{:S(2)}, u32[]{:S(2)}) collective-permute-start(bf16[48,1536]{1,0:T(8,128)(2,1)S(1)} %get-tuple-element.213), channel_id=1, source_target_pairs={{0,8},{1,9},{2,10},{3,11},{4,12},{5,13},{6,14},{7,15},{8,0},{9,1},... | collective-permute-start | bytes 442376 | tf_op jit(solution)/shard_map/ppermute | solution.py:252
  222.5 12.7 %collective-permute-start.47 = (bf16[2,64,768]{2,1,0:T(8,128)(2,1)S(1)}, bf16[2,64,768]{2,1,0:T(8,128)(2,1)S(1)}, u32[]{:S(2)}, u32[]{:S(2)}) collective-permute-start(bf16[2,64,768]{2,1,0:T(8,128)(2,1)S(1)} %copy-done.10), channel_id=1, source_target_pairs={{4,0},{5,1},{6,2},{7,3},{12,8},{13,9},{14,10},{15,11},{20,16},{21,... | collective-permute-start | bytes 589832 | tf_op jit(solution)/shard_map/ppermute | solution.py:252
  235.1 1.4 collective-permute-start.55
  (16 other events, 62.4 us)
where the time goes:
time: 239 us; the launch traced here: 238 us
  waiting for transfers between devices  101 us (42%)
  starting transfers between devices  75.7 us (32%)
  Pallas kernels  39.3 us (16%)
  other arithmetic  13.1 us (5%)
  local copies, waits for them, and re-layouts  7.03 us (3%)
    ppermute x60, waiting for transfers between devices, swap(): return lax.ppermute(array, ('head', 'blk'), pairs)  101 us
    ppermute x60, starting transfers between devices, swap(): return lax.ppermute(array, ('head', 'blk'), pairs)  75.7 us
    pallas_call x1, Pallas kernels, on_chip_pair(): call(backward_kernel, [SMEM] + [VMEM] * 11, [(VMEM, shaped((2, 64, WIDTH...  13.5 us
    pallas_call x1, Pallas kernels, on_chip_pair(): call(forward_kernel, [SMEM] + [VMEM] * 6, [(VMEM, shaped((ROWS, HALF))),...  12.7 us
  transfers between devices with their start and end apart: 60, of which 27 were waited for; matrix products, arithmetic and copies ran while one was open for 6% of the time, Pallas kernels for 16%

commit v1 on v0

--- a/solution.py
+++ b/solution.py
@@ -304,6 +304,12 @@
     return block, near, far, end
 
 
+def gather_z_twice(block):
+    near = swap(block, AXIS_Z_NEAR)
+    far = swap(jnp.stack([block, near]), AXIS_Z_FAR)
+    return block, near, far[0], far[1]
+
+
 def gather_first(four, cut):
     four_a = jnp.stack([array[:, :cut] for array in four])
     four_b = jnp.stack([array[:, cut:] for array in four])
@@ -350,6 +356,10 @@
 
 def fence(*arrays):
     return lax.optimization_barrier(arrays)
+
+
+def after(arrays, *others):
+    return fence(*arrays, *others)[: len(arrays)]
 
 
 def piece_rows(chip, which, pair, entry):
@@ -572,7 +582,7 @@
             d_rows[micro, at, :] = rows.astype(jnp.bfloat16)
             return carry
 
-        lax.fori_loop(0, POSITIONS // ROWS, row_chunk, 0)
+        lax.fori_loop(0, POSITIONS // ROWS, row_chunk, 0, unroll=4)
         own = d_rows[micro, pl.ds(first_row, 128), :].astype(jnp.float32)
         own = own + dot_nt(d_query[here, :], wqkv[:, :HALF])
         d_rows[micro, pl.ds(first_row, 128), :] = own.astype(jnp.bfloat16)
@@ -694,7 +704,6 @@
     ]
     wide = 3 * HALF + 128
     attn_four = gather_z(chip_block(core, *attn_halves))
-    attn_four = fence(*attn_four, got_x)[:4]
     attn_first = gather_first(attn_four, wide)
     up_block = chip_block(core, *split_units(w_up, 16))
     feed_blocks = [
@@ -703,12 +712,12 @@
         )
         for half in range(2)
     ]
-    four_0 = gather_z(fence(feed_blocks[0], *attn_four[1:])[0])
-    four_1 = gather_z(fence(feed_blocks[1], *four_0[1:])[0])
-    attn_pieces = gather_second(*attn_first)
-    first_0 = gather_first(fence(*four_0, *attn_first)[:4], WIDTH)
-    first_1 = gather_first(fence(*four_1, *first_0)[:4], WIDTH)
-    pieces_0 = gather_second(*first_0)
+    four_0 = gather_z_twice(*after((feed_blocks[0],), four))
+    four_1 = gather_z_twice(*after((feed_blocks[1],), *four_0[1:]))
+    attn_pieces = gather_second(*after(attn_first, *four_0))
+    first_0 = gather_first(after(four_0, got_x), WIDTH)
+    pieces_0 = gather_second(*after(first_0, *attn_pieces))
+    first_1 = gather_first(after(four_1, *first_0), WIDTH)
     cot_other = swap(cot, CORE)
     rows_shape = shaped((2, POSITIONS, WIDTH))
     attn, query, own_rows, gains, kv, normed_all, soft, wqkv, wout = call(
@@ -752,6 +761,8 @@
         weight_scratch,
         "feed_forward_and_back_first",
         20,
+        2 * 10**9,
+        10**6,
     )(
         ids, gains, attn, attn_other, own_rows, wout, wout_other, cot, cot_other, *pieces_0
     )
@@ -764,8 +775,8 @@
         weight_scratch,
         "feed_forward_and_back_second",
         20,
-        2 * 10**10,
-        10**8,
+        2 * 10**9,
+        10**6,
     )(ids, normed_two, cot_all, sum_mix, sum_norm, *pieces_1)
     part_other = swap(part, CORE)
     feed_0 = reduce_middle(*feed_0)
@@ -795,7 +806,7 @@
         wqkv, kv, soft,
     )
     mixed, d_residual, *outs = outs
-    outs, feed_0, feed_1 = fence(outs, feed_0, feed_1)
+    outs, feed_1 = fence(outs, feed_1)
     d_query, d_sum_half, keep_rows, send_rows, d_kv = outs
     feed_0 = reduce_z(*feed_0)
     feed_1 = reduce_middle(*feed_1)
@@ -810,6 +821,8 @@
         ],
         "attention_weight_gradients",
         20,
+        2 * 10**10,
+        10**8,
     )(ids, attn_all, d_sum_half, d_query, d_kv, normed_all)
     keep_rows, got_rows, grad_attn_pieces, feed_1 = fence(
         keep_rows, got_rows, grad_attn_pieces, feed_1
@@ -817,7 +830,7 @@
     crossed = swap(add(keep_rows[4:], got_rows[4:]).astype(bf), AXIS_X)
     attn_first = reduce_start(grad_attn_pieces)
     feed_1 = reduce_z(*feed_1)
-    feed_1, crossed, attn_first = fence(feed_1, crossed, attn_first)
+    feed_0, feed_1, crossed = fence(feed_0, feed_1, crossed)
     rows_4 = add(keep_rows[:4], got_rows[:4], crossed).astype(bf)
     to_near = swap(rows_4[1], AXIS_Z_NEAR, downward(AXIS_Z_NEAR))
     to_far = swap(rows_4[2], AXIS_Z_FAR, downward(AXIS_Z_FAR))

time: 239 us -> 226 us (0.946)
  waiting for transfers between devices: 101 us -> 82 us
  starting transfers between devices: 75.7 us -> 84.7 us
    ppermute x60 -> x58, waiting for transfers between devices: 101 us -> 82 us  [swap(): return lax.ppermute(array, ('head', 'blk'), pairs)]
    ppermute x60 -> x58, starting transfers between devices: 75.7 us -> 84.7 us  [swap(): return lax.ppermute(array, ('head', 'blk'), pairs)]
  transfers between devices with their start and end apart: 60 -> 58, of which waited for: 27 -> 26; matrix products, arithmetic and copies ran while one was open for 6% -> 7% of each run, Pallas kernels for 16% -> 17%
where the time goes in v1:
time: 226 us; the launch traced here: 225 us
  starting transfers between devices  84.7 us (37%)
  waiting for transfers between devices  82 us (36%)
  Pallas kernels  37.5 us (17%)
  other arithmetic  11.7 us (5%)
  local copies, waits for them, and re-layouts  7.76 us (3%)
    ppermute x58, starting transfers between devices, swap(): return lax.ppermute(array, ('head', 'blk'), pairs)  84.7 us
    ppermute x58, waiting for transfers between devices, swap(): return lax.ppermute(array, ('head', 'blk'), pairs)  82 us
    pallas_call x1, Pallas kernels, on_chip_pair(): call(forward_kernel, [SMEM] + [VMEM] * 6, [(VMEM, shaped((ROWS, HALF))),...  12.7 us
    pallas_call x1, Pallas kernels, on_chip_pair(): call(backward_kernel, [SMEM] + [VMEM] * 11, [(VMEM, shaped((2, 64, WIDTH...  11.9 us
  transfers between devices with their start and end apart: 58, of which 26 were waited for; matrix products, arithmetic and copies ran while one was open for 7% of the time, Pallas kernels for 17%

profile of v1, /device:TPU:0, one launch (start us, length us, event | category | flops | bytes accessed | tf_op | source)
XLA Modules:
  0.0 225.3 jit_solution(16045587957114607763)
XLA Ops:
  1.5 1.0 constant_dynamic-update-slice_fusion.4
  2.5 7.0 %collective-permute-start.2 = (bf16[2,64,768]{2,1,0:T(8,128)(2,1)S(1)}, bf16[2,64,768]{2,1,0:T(8,128)(2,1)S(1)}, u32[]{:S(2)}, u32[]{:S(2)}) collective-permute-start(bf16[2,64,768]{2,1,0:T(8,128)(2,1)S(1)} %get-tuple-element.199.tokens), channel_id=1, source_target_pairs={{0,12},{1,13},{2,14},{3,15},{4,8},{5,9},{6,10},{7,11},{16,28},{17,... | collective-permute-start | bytes 589832 | tf_op jit(solution)/shard_map/ppermute | solution.py:252
  9.5 1.3 collective-permute-start.1
  10.8 2.5 %collective-permute-start = (bf16[2,64,768]{2,1,0:T(8,128)(2,1)S(1)}, bf16[2,64,768]{2,1,0:T(8,128)(2,1)S(1)}, u32[]{:S(2)}, u32[]{:S(2)}) collective-permute-start(bf16[2,64,768]{2,1,0:T(8,128)(2,1)S(1)} %get-tuple-element.199.tokens), channel_id=1, source_target_pairs={{0,4},{1,5},{2,6},{3,7},{8,12},{9,13},{10,14},{11,15},{16,20},{17,... | collective-permute-start | bytes 589832 | tf_op jit(solution)/shard_map/ppermute | solution.py:252
  19.6 4.4 %collective-permute-start.8 = (bf16[48,1664]{1,0:T(8,128)(2,1)S(1)}, bf16[48,1664]{1,0:T(8,128)(2,1)S(1)}, u32[]{:S(2)}, u32[]{:S(2)}) collective-permute-start(bf16[48,1664]{1,0:T(8,128)(2,1)S(1)} %pad_maximum_fusion.10), channel_id=1, source_target_pairs={{0,12},{1,13},{2,14},{3,15},{4,8},{5,9},{6,10},{7,11},{8,4},{9,5},... | collective-permute-start | bytes 479240 | tf_op jit(solution)/shard_map/ppermute | solution.py:252
  24.0 1.6 collective-permute-start.3
  25.6 6.9 %collective-permute-start.12 = (bf16[48,1536]{1,0:T(8,128)(2,1)S(1)}, bf16[48,1536]{1,0:T(8,128)(2,1)S(1)}, u32[]{:S(2)}, u32[]{:S(2)}) collective-permute-start(bf16[48,1536]{1,0:T(8,128)(2,1)S(1)} %pad_maximum_fusion.18), channel_id=1, source_target_pairs={{0,4},{1,5},{2,6},{3,7},{4,0},{5,1},{6,2},{7,3},{8,12},{9,13},{10,... | collective-permute-start | bytes 442376 | tf_op jit(solution)/shard_map/ppermute | solution.py:252
  33.7 1.6 collective-permute-start.9
  35.9 7.3 %collective-permute-start.13 = (bf16[2,48,1536]{2,1,0:T(8,128)(2,1)S(1)}, bf16[2,48,1536]{2,1,0:T(8,128)(2,1)S(1)}, u32[]{:S(2)}, u32[]{:S(2)}) collective-permute-start(bf16[2,48,1536]{2,1,0:T(8,128)(2,1)S(1)} %pad_maximum_fusion.4), channel_id=1, source_target_pairs={{0,8},{1,9},{2,10},{3,11},{4,12},{5,13},{6,14},{7,15},{8,0},{9,1},... | collective-permute-start | bytes 884744 | tf_op jit(solution)/shard_map/ppermute | solution.py:252
  43.3 1.6 collective-permute-start.10
  44.8 10.6 %collective-permute-done.13 = bf16[2,48,1536]{2,1,0:T(8,128)(2,1)S(1)} collective-permute-done((bf16[2,48,1536]{2,1,0:T(8,128)(2,1)S(1)}, bf16[2,48,1536]{2,1,0:T(8,128)(2,1)S(1)}, u32[]{:S(2)}, u32[]{:S(2)}) %collective-permute-start.13) | collective-permute-done | bytes 294944 | tf_op jit(solution)/shard_map/ppermute | solution.py:252
  55.6 1.3 collective-permute-start.15
  56.9 1.6 collective-permute-start.14
  58.5 2.6 %collective-permute-done.23 = bf16[48,1536]{1,0:T(8,128)(2,1)S(1)} collective-permute-done((bf16[48,1536]{1,0:T(8,128)(2,1)S(1)}, bf16[48,1536]{1,0:T(8,128)(2,1)S(1)}, u32[]{:S(2)}, u32[]{:S(2)}) %collective-permute-start.23) | collective-permute-done | bytes 147488 | tf_op jit(solution)/shard_map/ppermute | solution.py:252
  62.1 2.3 %collective-permute-start.19 = (bf16[4,48,768]{2,1,0:T(8,128)(2,1)S(1)}, bf16[4,48,768]{2,1,0:T(8,128)(2,1)S(1)}, u32[]{:S(2)}, u32[]{:S(2)}) collective-permute-start(bf16[4,48,768]{2,1,0:T(8,128)(2,1)S(1)} %pad_maximum_fusion.5), channel_id=1, source_target_pairs={{0,2},{1,3},{2,0},{3,1},{4,6},{5,7},{6,4},{7,5},{8,10},{9,11},{10,... | collective-permute-start | bytes 884744 | tf_op jit(solution)/shard_map/ppermute | solution.py:252
  64.4 1.6 collective-permute-start.20
  66.0 10.3 %collective-permute-done.24 = bf16[2,48,1536]{2,1,0:T(8,128)(2,1)S(1)} collective-permute-done((bf16[2,48,1536]{2,1,0:T(8,128)(2,1)S(1)}, bf16[2,48,1536]{2,1,0:T(8,128)(2,1)S(1)}, u32[]{:S(2)}, u32[]{:S(2)}) %collective-permute-start.24) | collective-permute-done | bytes 294944 | tf_op jit(solution)/shard_map/ppermute | solution.py:252
  76.4 10.0 %collective-permute-done.20 = bf16[4,48,768]{2,1,0:T(8,128)(2,1)S(1)} collective-permute-done((bf16[4,48,768]{2,1,0:T(8,128)(2,1)S(1)}, bf16[4,48,768]{2,1,0:T(8,128)(2,1)S(1)}, u32[]{:S(2)}, u32[]{:S(2)}) %collective-permute-start.20) | collective-permute-done | bytes 294944 | tf_op jit(solution)/shard_map/ppermute | solution.py:252
  86.5 1.1 collective-permute-start.25
  87.6 1.6 collective-permute-start.27
  89.3 1.1 collective-permute-start.22
  91.1 12.7 %attention_forward.1 = (bf16[256,384]{1,0:T(8,128)(2,1)S(1)}, bf16[256,384]{1,0:T(8,128)(2,1)S(1)}, bf16[256,768]{1,0:T(8,128)(2,1)S(1)}, f32[8,768]{1,0:T(8,128...) custom-call(s32[2]{0:T(128)S(1)} %pad_add_fusion.ids, ...), custom_call_target="tpu_custom_call" | custom-call | tf_op jit(solution)/shard_map/attention_forward/pallas_call | solution.py:723
  104.4 1.6 collective-permute-start.26
  106.1 1.0 collective-permute-start.28
  108.5 4.2 %feed_forward_and_back_first.1 = (bf16[256,768]{1,0:T(8,128)(2,1)S(1)}, bf16[256,768]{1,0:T(8,128)(2,1)S(1)}, f32[256,768]{1,0:T(8,128)S(1)}, bf16[256,768]{1,0:...) custom-call(s32[2]{0:T(128)S(1)} %pad_add_fusion.ids, ...), custom_call_target="tpu_custom_call" | custom-call | flops 2000000000 | bytes 1000000 | tf_op jit(solution)/shard_map/feed_forward_and_back_first/pallas_call | solution.py:749
  112.7 1.6 collective-permute-start.35
  114.3 1.0 collective-permute-start.37
  115.3 5.4 %collective-permute-done.26.w1 = bf16[8,48,768]{2,1,0:T(8,128)(2,1)S(1)} collective-permute-done((bf16[8,48,768]{2,1,0:T(8,128)(2,1)S(1)}, bf16[8,48,768]{2,1,0:T(8,128)(2,1)S(1)}, u32[]{:S(2)}, u32[]{:S(2)}) %collective-permute-start.26) | collective-permute-done | bytes 589856 | tf_op jit(solution)/shard_map/ppermute | solution.py:252
  120.7 1.6 collective-permute-done.28.w3
  122.3 3.6 %feed_forward_and_back_second.1 = (bf16[512,768]{1,0:T(8,128)(2,1)S(1)}, bf16[8,48,768]{2,1,0:T(8,128)(2,1)S(1)}, bf16[8,48,768]{2,1,0:T(8,128)(2,1)S(1)}, bf16[...) custom-call(s32[2]{0:T(128)S(1)} %pad_add_fusion.ids, bf16[256,768]{1,0:T(8,128)(2,1)S(1)} %get-tuple-element.109.normed, ...), custom_call_target="tpu_custom_call" | custom-call | flops 2000000000 | bytes 1000000 | tf_op jit(solution)/shard_map/feed_forward_and_back_second/pallas_call | solution.py:771
  126.0 1.6 collective-permute-start.30
  127.5 1.0 collective-permute-start.31
  128.5 4.9 %collective-permute-done.35 = bf16[8,48,768]{2,1,0:T(8,128)(2,1)S(1)} collective-permute-done((bf16[8,48,768]{2,1,0:T(8,128)(2,1)S(1)}, bf16[8,48,768]{2,1,0:T(8,128)(2,1)S(1)}, u32[]{:S(2)}, u32[]{:S(2)}) %collective-permute-start.35) | collective-permute-done | bytes 589856 | tf_op jit(solution)/shard_map/ppermute | solution.py:252
  133.4 1.0 collective-permute-start.36
  135.0 1.5 collective-permute-start.38
  136.5 11.9 %attention_backward.1 = (bf16[2,64,767]{2,1,0:T(8,128)(2,1)}, f32[2,64,768]{2,1,0:T(8,128)S(1)}, bf16[256,384]{1,0:T(8,128)(2,1)S(1)}, bf16[256,384]{1,0:T(8,128...) custom-call(s32[2]{0:T(128)S(1)} %pad_add_fusion.ids, ...), custom_call_target="tpu_custom_call" | custom-call | tf_op jit(solution)/shard_map/attention_backward/pallas_call | solution.py:784
  150.0 1.0 collective-permute-start.33
  151.0 4.0 %attention_weight_gradients.1 = (bf16[8,48,1152]{2,1,0:T(8,128)(2,1)S(1)}, bf16[8,48,1152]{2,1,0:T(8,128)(2,1)S(1)}, bf16[8,48,384]{2,1,0:T(8,128)(2,1)S(1)}, bf16[8,48,384]{2,1,0:T(8,128)(2,1)S(1)}) custom-call(s32[2]{0:T(128)S(1)} %pad_add_fusion.ids, bf16[256,768]{1,0:T(8,128)(2,1)S(1)} %get-tuple-element.135.attn, ...), custom_call_target="tpu_custom_call" | custom-call | flops 20000000000 | bytes 100000000 | tf_op jit(solution)/shard_map/attention_weight_gradients/pallas_call | solution.py:814
  155.3 4.2 %collective-permute-start.41 = (bf16[48,1536]{1,0:T(8,128)(2,1)S(1)}, bf16[48,1536]{1,0:T(8,128)(2,1)S(1)}, u32[]{:S(2)}, u32[]{:S(2)}) collective-permute-start(bf16[48,1536]{1,0:T(8,128)(2,1)S(1)} %get-tuple-element.211), channel_id=1, source_target_pairs={{0,12},{1,13},{2,14},{3,15},{4,8},{5,9},{6,10},{7,11},{8,4},{9,5},... | collective-permute-start | bytes 442376 | tf_op jit(solution)/shard_map/ppermute | solution.py:252
  159.6 1.5 collective-permute-start.40
  161.0 1.4 collective-permute-start.51
  163.6 7.4 %collective-permute-done.51 = bf16[8,48,384]{2,1,0:T(8,128)(2,1)S(1)} collective-permute-done((bf16[8,48,384]{2,1,0:T(8,128)(2,1)S(1)}, bf16[8,48,384]{2,1,0:T(8,128)(2,1)S(1)}, u32[]{:S(2)}, u32[]{:S(2)}) %collective-permute-start.51) | collective-permute-done | bytes 294944 | tf_op jit(solution)/shard_map/ppermute | solution.py:252
  171.1 1.6 collective-permute-start.52
  172.7 3.0 %collective-permute-start.44 = (bf16[48,1536]{1,0:T(8,128)(2,1)S(1)}, bf16[48,1536]{1,0:T(8,128)(2,1)S(1)}, u32[]{:S(2)}, u32[]{:S(2)}) collective-permute-start(bf16[48,1536]{1,0:T(8,128)(2,1)S(1)} %get-tuple-element.207), channel_id=1, source_target_pairs={{0,12},{1,13},{2,14},{3,15},{4,8},{5,9},{6,10},{7,11},{8,4},{9,5},... | collective-permute-start | bytes 442376 | tf_op jit(solution)/shard_map/ppermute | solution.py:252
  176.3 1.6 collective-permute-start.43
  178.0 2.0 collective-permute-start.49
  180.6 1.7 collective-permute-done.42
  182.3 3.4 %collective-permute-done.43 = bf16[48,1536]{1,0:T(8,128)(2,1)S(1)} collective-permute-done((bf16[48,1536]{1,0:T(8,128)(2,1)S(1)}, bf16[48,1536]{1,0:T(8,128)(2,1)S(1)}, u32[]{:S(2)}, u32[]{:S(2)}) %collective-permute-start.43) | collective-permute-done | bytes 147488 | tf_op jit(solution)/shard_map/ppermute | solution.py:252
  187.2 1.3 collective-permute-start.48
  188.4 1.3 collective-permute-start.47
  190.8 5.4 %collective-permute-done.49 = bf16[8,48,1152]{2,1,0:T(8,128)(2,1)S(1)} collective-permute-done((bf16[8,48,1152]{2,1,0:T(8,128)(2,1)S(1)}, bf16[8,48,1152]{2,1,0:T(8,128)(2,1)S(1)}, u32[]{:S(2)}, u32[]{:S(2)}) %collective-permute-start.49) | collective-permute-done | bytes 884768 | tf_op jit(solution)/shard_map/ppermute | solution.py:252
  196.2 1.0 add_convert_fusion.3
  197.2 1.6 collective-permute-start.50
  199.7 1.1 reshape.60
  200.8 1.2 multiply_reduce_fusion
  202.0 3.7 %collective-permute-done.50 = bf16[4,48,1152]{2,1,0:T(8,128)(2,1)} collective-permute-done((bf16[4,48,1152]{2,1,0:T(8,128)(2,1)}, bf16[4,48,1152]{2,1,0:T(8,128)(2,1)}, u32[]{:S(2)}, u32[]{:S(2)}) %collective-permute-start.50) | collective-permute-done | bytes 442400 | tf_op jit(solution)/shard_map/ppermute | solution.py:252
  205.8 1.3 add_convert_fusion.2
  207.1 1.7 collective-permute-start.53
  208.8 2.3 %collective-permute-start.55 = (bf16[48,1536]{1,0:T(8,128)(2,1)S(1)}, bf16[48,1536]{1,0:T(8,128)(2,1)S(1)}, u32[]{:S(2)}, u32[]{:S(2)}) collective-permute-start(bf16[48,1536]{1,0:T(8,128)(2,1)S(1)} %get-tuple-element.205), channel_id=1, source_target_pairs={{0,12},{1,13},{2,14},{3,15},{4,8},{5,9},{6,10},{7,11},{8,4},{9,5},... | collective-permute-start | bytes 442376 | tf_op jit(solution)/shard_map/ppermute | solution.py:252
  211.7 2.1 collective-permute-done.53
  213.8 1.3 collective-permute-start.46
  215.1 3.4 %collective-permute-done.55 = bf16[48,1536]{1,0:T(8,128)(2,1)S(1)} collective-permute-done((bf16[48,1536]{1,0:T(8,128)(2,1)S(1)}, bf16[48,1536]{1,0:T(8,128)(2,1)S(1)}, u32[]{:S(2)}, u32[]{:S(2)}) %collective-permute-start.55) | collective-permute-done | bytes 147488 | tf_op jit(solution)/shard_map/ppermute | solution.py:252
  218.5 2.9 %collective-permute-done.54 = bf16[48,1536]{1,0:T(8,128)(2,1)S(1)} collective-permute-done((bf16[48,1536]{1,0:T(8,128)(2,1)S(1)}, bf16[48,1536]{1,0:T(8,128)(2,1)S(1)}, u32[]{:S(2)}, u32[]{:S(2)}) %collective-permute-start.54) | collective-permute-done | bytes 147488 | tf_op jit(solution)/shard_map/ppermute | solution.py:252
  222.3 1.2 token_gradient.1
  (207 shorter events, 24.7 us)
Async XLA Ops:
  0.6 14.6 %copy-start.10 = (bf16[24,767]{1,0:T(8,128)(2,1)S(1)}, bf16[24,767]{1,0:T(8,128)(2,1)}, u32[]{:S(2)}) copy-start(bf16[24,767]{1,0:T(8,128)(2,1)} %param.13) | copy-start | bytes 110452
  0.6 15.3 %copy-start.4 = (bf16[24,3072]{1,0:T(8,128)(2,1)S(1)}, bf16[24,3072]{1,0:T(8,128)(2,1)}, u32[]{:S(2)}) copy-start(bf16[24,3072]{1,0:T(8,128)(2,1)} %param.14) | copy-start | bytes 442372
  2.5 17.1 %collective-permute-start.2 = (bf16[2,64,768]{2,1,0:T(8,128)(2,1)S(1)}, bf16[2,64,768]{2,1,0:T(8,128)(2,1)S(1)}, u32[]{:S(2)}, u32[]{:S(2)}) collective-permute-start(bf16[2,64,768]{2,1,0:T(8,128)(2,1)S(1)} %get-tuple-element.199.tokens), channel_id=1, source_target_pairs={{0,12},{1,13},{2,14},{3,15},{4,8},{5,9},{6,10},{7,11},{16,28},{17,... | collective-permute-start | bytes 589832 | tf_op jit(solution)/shard_map/ppermute | solution.py:252
  9.5 14.4 %collective-permute-start.1 = (bf16[2,64,768]{2,1,0:T(8,128)(2,1)S(1)}, bf16[2,64,768]{2,1,0:T(8,128)(2,1)S(1)}, u32[]{:S(2)}, u32[]{:S(2)}) collective-permute-start(bf16[2,64,768]{2,1,0:T(8,128)(2,1)S(1)} %get-tuple-element.199.tokens), channel_id=1, source_target_pairs={{0,8},{1,9},{2,10},{3,11},{4,12},{5,13},{6,14},{7,15},{16,24},{17,... | collective-permute-start | bytes 589832 | tf_op jit(solution)/shard_map/ppermute | solution.py:252
  10.8 13.1 %collective-permute-start = (bf16[2,64,768]{2,1,0:T(8,128)(2,1)S(1)}, bf16[2,64,768]{2,1,0:T(8,128)(2,1)S(1)}, u32[]{:S(2)}, u32[]{:S(2)}) collective-permute-start(bf16[2,64,768]{2,1,0:T(8,128)(2,1)S(1)} %get-tuple-element.199.tokens), channel_id=1, source_target_pairs={{0,4},{1,5},{2,6},{3,7},{8,12},{9,13},{10,14},{11,15},{16,20},{17,... | collective-permute-start | bytes 589832 | tf_op jit(solution)/shard_map/ppermute | solution.py:252
  16.0 3.3 %collective-permute-start.5 = (bf16[24,1664]{1,0:T(8,128)(2,1)}, bf16[24,1664]{1,0:T(8,128)(2,1)S(1)}, u32[]{:S(2)}, u32[]{:S(2)}) collective-permute-start(bf16[24,1664]{1,0:T(8,128)(2,1)} %broadcast_select_fusion.2), channel_id=1, source_target_pairs={{0,1},{1,0},{2,3},{3,2},{4,5},{5,4},{6,7},{7,6},{8,9},{9,8},{10,11... | collective-permute-start | bytes 239624 | tf_op jit(solution)/shard_map/ppermute | solution.py:252
  17.6 1.6 collective-permute-start.11
  19.4 13.2 %collective-permute-start.7 = (bf16[48,1664]{1,0:T(8,128)(2,1)S(1)}, bf16[48,1664]{1,0:T(8,128)(2,1)S(1)}, u32[]{:S(2)}, u32[]{:S(2)}) collective-permute-start(bf16[48,1664]{1,0:T(8,128)(2,1)S(1)} %pad_maximum_fusion.10), channel_id=1, source_target_pairs={{0,8},{1,9},{2,10},{3,11},{4,12},{5,13},{6,14},{7,15},{8,0},{9,1},... | collective-permute-start | bytes 479240 | tf_op jit(solution)/shard_map/ppermute | solution.py:252
  19.5 13.4 %collective-permute-start.6 = (bf16[48,1664]{1,0:T(8,128)(2,1)S(1)}, bf16[48,1664]{1,0:T(8,128)(2,1)S(1)}, u32[]{:S(2)}, u32[]{:S(2)}) collective-permute-start(bf16[48,1664]{1,0:T(8,128)(2,1)S(1)} %pad_maximum_fusion.10), channel_id=1, source_target_pairs={{0,4},{1,5},{2,6},{3,7},{4,0},{5,1},{6,2},{7,3},{8,12},{9,13},{10,... | collective-permute-start | bytes 479240 | tf_op jit(solution)/shard_map/ppermute | solution.py:252
  19.6 14.0 %collective-permute-start.8 = (bf16[48,1664]{1,0:T(8,128)(2,1)S(1)}, bf16[48,1664]{1,0:T(8,128)(2,1)S(1)}, u32[]{:S(2)}, u32[]{:S(2)}) collective-permute-start(bf16[48,1664]{1,0:T(8,128)(2,1)S(1)} %pad_maximum_fusion.10), channel_id=1, source_target_pairs={{0,12},{1,13},{2,14},{3,15},{4,8},{5,9},{6,10},{7,11},{8,4},{9,5},... | collective-permute-start | bytes 479240 | tf_op jit(solution)/shard_map/ppermute | solution.py:252
  24.0 38.0 %collective-permute-start.3 = (bf16[4,2,64,768]{3,2,1,0:T(8,128)(2,1)S(1)}, bf16[4,2,64,768]{3,2,1,0:T(8,128)(2,1)S(1)}, u32[]{:S(2)}, u32[]{:S(2)}) collective-permute-start(bf16[4,2,64,768]{3,2,1,0:T(8,128)(2,1)S(1)} %pad_maximum_fusion), channel_id=1, source_target_pairs={{0,2},{1,3},{2,0},{3,1},{4,6},{5,7},{6,4},{7,5},{8,10},{9,11},{10,... | collective-permute-start | bytes 2359304 | tf_op jit(solution)/shard_map/ppermute | solution.py:252
  25.6 10.3 %collective-permute-start.12 = (bf16[48,1536]{1,0:T(8,128)(2,1)S(1)}, bf16[48,1536]{1,0:T(8,128)(2,1)S(1)}, u32[]{:S(2)}, u32[]{:S(2)}) collective-permute-start(bf16[48,1536]{1,0:T(8,128)(2,1)S(1)} %pad_maximum_fusion.18), channel_id=1, source_target_pairs={{0,4},{1,5},{2,6},{3,7},{4,0},{5,1},{6,2},{7,3},{8,12},{9,13},{10,... | collective-permute-start | bytes 442376 | tf_op jit(solution)/shard_map/ppermute | solution.py:252
  33.7 21.8 %collective-permute-start.9 = (bf16[4,48,1280]{2,1,0:T(8,128)(2,1)S(1)}, bf16[4,48,1280]{2,1,0:T(8,128)(2,1)S(1)}, u32[]{:S(2)}, u32[]{:S(2)}) collective-permute-start(bf16[4,48,1280]{2,1,0:T(8,128)(2,1)S(1)} %pad_maximum_fusion.2), channel_id=1, source_target_pairs={{0,2},{1,3},{2,0},{3,1},{4,6},{5,7},{6,4},{7,5},{8,10},{9,11},{10,... | collective-permute-start | bytes 1474568 | tf_op jit(solution)/shard_map/ppermute | solution.py:252
  35.9 19.5 %collective-permute-start.13 = (bf16[2,48,1536]{2,1,0:T(8,128)(2,1)S(1)}, bf16[2,48,1536]{2,1,0:T(8,128)(2,1)S(1)}, u32[]{:S(2)}, u32[]{:S(2)}) collective-permute-start(bf16[2,48,1536]{2,1,0:T(8,128)(2,1)S(1)} %pad_maximum_fusion.4), channel_id=1, source_target_pairs={{0,8},{1,9},{2,10},{3,11},{4,12},{5,13},{6,14},{7,15},{8,0},{9,1},... | collective-permute-start | bytes 884744 | tf_op jit(solution)/shard_map/ppermute | solution.py:252
  43.3 12.2 %collective-permute-start.10 = (bf16[4,48,384]{2,1,0:T(8,128)(2,1)S(1)}, bf16[4,48,384]{2,1,0:T(8,128)(2,1)S(1)}, u32[]{:S(2)}, u32[]{:S(2)}) collective-permute-start(bf16[4,48,384]{2,1,0:T(8,128)(2,1)S(1)} %pad_maximum_fusion.17), channel_id=1, source_target_pairs={{0,16},{1,17},{2,18},{3,19},{4,20},{5,21},{6,22},{7,23},{8,24},{9,... | collective-permute-start | bytes 442376 | tf_op jit(solution)/shard_map/ppermute | solution.py:252
  55.4 5.7 %collective-permute-start.23 = (bf16[48,1536]{1,0:T(8,128)(2,1)S(1)}, bf16[48,1536]{1,0:T(8,128)(2,1)S(1)}, u32[]{:S(2)}, u32[]{:S(2)}) collective-permute-start(bf16[48,1536]{1,0:T(8,128)(2,1)S(1)} %fusion.24), channel_id=1, source_target_pairs={{0,4},{1,5},{2,6},{3,7},{4,0},{5,1},{6,2},{7,3},{8,12},{9,13},{10,... | collective-permute-start | bytes 442376 | tf_op jit(solution)/shard_map/ppermute | solution.py:252
  55.6 33.7 %collective-permute-start.15 = (bf16[8,48,384]{2,1,0:T(8,128)(2,1)S(1)}, bf16[8,48,384]{2,1,0:T(8,128)(2,1)S(1)}, u32[]{:S(2)}, u32[]{:S(2)}) collective-permute-start(bf16[8,48,384]{2,1,0:T(8,128)(2,1)S(1)} %constant_dynamic-update-slice_fusion.17.w2), channel_id=1, source_target_pairs={{0,2},{1,3},{2,0},{3,1},{4,6},{5,7},{6,4},{7,5},{8,10},{9,11},{10,... | collective-permute-start | bytes 884744 | tf_op jit(solution)/shard_map/ppermute | solution.py:252
  56.9 32.3 %collective-permute-start.14 = (bf16[8,48,1280]{2,1,0:T(8,128)(2,1)S(1)}, bf16[8,48,1280]{2,1,0:T(8,128)(2,1)S(1)}, u32[]{:S(2)}, u32[]{:S(2)}) collective-permute-start(bf16[8,48,1280]{2,1,0:T(8,128)(2,1)S(1)} %constant_dynamic-update-slice_fusion.15.w0), channel_id=1, source_target_pairs={{0,16},{1,17},{2,18},{3,19},{4,20},{5,21},{6,22},{7,23},{8,24},{9,... | collective-permute-start | bytes 2949128 | tf_op jit(solution)/shard_map/ppermute | solution.py:252
  61.1 15.2 %collective-permute-start.24 = (bf16[2,48,1536]{2,1,0:T(8,128)(2,1)S(1)}, bf16[2,48,1536]{2,1,0:T(8,128)(2,1)S(1)}, u32[]{:S(2)}, u32[]{:S(2)}) collective-permute-start(bf16[2,48,1536]{2,1,0:T(8,128)(2,1)S(1)} %pad_maximum_fusion.7), channel_id=1, source_target_pairs={{0,8},{1,9},{2,10},{3,11},{4,12},{5,13},{6,14},{7,15},{8,0},{9,1},... | collective-permute-start | bytes 884744 | tf_op jit(solution)/shard_map/ppermute | solution.py:252
  62.1 14.3 %collective-permute-start.19 = (bf16[4,48,768]{2,1,0:T(8,128)(2,1)S(1)}, bf16[4,48,768]{2,1,0:T(8,128)(2,1)S(1)}, u32[]{:S(2)}, u32[]{:S(2)}) collective-permute-start(bf16[4,48,768]{2,1,0:T(8,128)(2,1)S(1)} %pad_maximum_fusion.5), channel_id=1, source_target_pairs={{0,2},{1,3},{2,0},{3,1},{4,6},{5,7},{6,4},{7,5},{8,10},{9,11},{10,... | collective-permute-start | bytes 884744 | tf_op jit(solution)/shard_map/ppermute | solution.py:252
  64.4 22.0 %collective-permute-start.20 = (bf16[4,48,768]{2,1,0:T(8,128)(2,1)S(1)}, bf16[4,48,768]{2,1,0:T(8,128)(2,1)S(1)}, u32[]{:S(2)}, u32[]{:S(2)}) collective-permute-start(bf16[4,48,768]{2,1,0:T(8,128)(2,1)S(1)} %pad_maximum_fusion.6), channel_id=1, source_target_pairs={{0,16},{1,17},{2,18},{3,19},{4,20},{5,21},{6,22},{7,23},{8,24},{9,... | collective-permute-start | bytes 884744 | tf_op jit(solution)/shard_map/ppermute | solution.py:252
  76.3 14.7 %collective-permute-start.4 = (bf16[8,2,64,768]{3,2,1,0:T(8,128)(2,1)S(1)}, bf16[8,2,64,768]{3,2,1,0:T(8,128)(2,1)S(1)}, u32[]{:S(2)}, u32[]{:S(2)}) collective-permute-start(bf16[8,2,64,768]{3,2,1,0:T(8,128)(2,1)S(1)} %constant_dynamic-update-slice_fusion.tok_mine), channel_id=1, source_target_pairs={{0,1},{1,0},{2,3},{3,2},{4,5},{5,4},{6,7},{7,6},{8,9},{9,8},{10,11... | collective-permute-start | bytes 4718600 | tf_op jit(solution)/shard_map/ppermute | solution.py:252
  86.5 17.3 %collective-permute-start.25 = (bf16[4,48,768]{2,1,0:T(8,128)(2,1)S(1)}, bf16[4,48,768]{2,1,0:T(8,128)(2,1)S(1)}, u32[]{:S(2)}, u32[]{:S(2)}) collective-permute-start(bf16[4,48,768]{2,1,0:T(8,128)(2,1)S(1)} %pad_maximum_fusion.8), channel_id=1, source_target_pairs={{0,2},{1,3},{2,0},{3,1},{4,6},{5,7},{6,4},{7,5},{8,10},{9,11},{10,... | collective-permute-start | bytes 884744 | tf_op jit(solution)/shard_map/ppermute | solution.py:252
  87.6 16.8 %collective-permute-start.27 = (bf16[4,48,768]{2,1,0:T(8,128)(2,1)S(1)}, bf16[4,48,768]{2,1,0:T(8,128)(2,1)S(1)}, u32[]{:S(2)}, u32[]{:S(2)}) collective-permute-start(bf16[4,48,768]{2,1,0:T(8,128)(2,1)S(1)} %pad_maximum_fusion.9), channel_id=1, source_target_pairs={{0,16},{1,17},{2,18},{3,19},{4,20},{5,21},{6,22},{7,23},{8,24},{9,... | collective-permute-start | bytes 884744 | tf_op jit(solution)/shard_map/ppermute | solution.py:252
  89.3 17.8 %collective-permute-start.22 = (bf16[8,48,768]{2,1,0:T(8,128)(2,1)S(1)}, bf16[8,48,768]{2,1,0:T(8,128)(2,1)S(1)}, u32[]{:S(2)}, u32[]{:S(2)}) collective-permute-start(bf16[8,48,768]{2,1,0:T(8,128)(2,1)S(1)} %constant_dynamic-update-slice_fusion.21.w2), channel_id=1, source_target_pairs={{0,2},{1,3},{2,0},{3,1},{4,6},{5,7},{6,4},{7,5},{8,10},{9,11},{10,... | collective-permute-start | bytes 1769480 | tf_op jit(solution)/shard_map/ppermute | solution.py:252
  90.5 17.6 %collective-permute-start.21 = (bf16[8,48,768]{2,1,0:T(8,128)(2,1)S(1)}, bf16[8,48,768]{2,1,0:T(8,128)(2,1)S(1)}, u32[]{:S(2)}, u32[]{:S(2)}) collective-permute-start(bf16[8,48,768]{2,1,0:T(8,128)(2,1)S(1)} %constant_dynamic-update-slice_fusion.19.w0), channel_id=1, source_target_pairs={{0,16},{1,17},{2,18},{3,19},{4,20},{5,21},{6,22},{7,23},{8,24},{9,... | collective-permute-start | bytes 1769480 | tf_op jit(solution)/shard_map/ppermute | solution.py:252
  103.7 4.8 %collective-permute-start.17 = (bf16[768,384]{1,0:T(8,128)(2,1)S(1)}, bf16[768,384]{1,0:T(8,128)(2,1)S(1)}, u32[]{:S(2)}, u32[]{:S(2)}) collective-permute-start(bf16[768,384]{1,0:T(8,128)(2,1)S(1)} %get-tuple-element.99.wout_mine), channel_id=1, source_target_pairs={{0,1},{1,0},{2,3},{3,2},{4,5},{5,4},{6,7},{7,6},{8,9},{9,8},{10,11... | collective-permute-start | bytes 1769480 | tf_op jit(solution)/shard_map/ppermute | solution.py:252
  103.8 2.2 collective-permute-start.18
  104.4 16.3 %collective-permute-start.26 = (bf16[8,48,768]{2,1,0:T(8,128)(2,1)S(1)}, bf16[8,48,768]{2,1,0:T(8,128)(2,1)S(1)}, u32[]{:S(2)}, u32[]{:S(2)}) collective-permute-start(bf16[8,48,768]{2,1,0:T(8,128)(2,1)S(1)} %constant_dynamic-update-slice_fusion.23.w0), channel_id=1, source_target_pairs={{0,16},{1,17},{2,18},{3,19},{4,20},{5,21},{6,22},{7,23},{8,24},{9,... | collective-permute-start | bytes 1769480 | tf_op jit(solution)/shard_map/ppermute | solution.py:252
  106.1 16.2 %collective-permute-start.28 = (bf16[8,48,768]{2,1,0:T(8,128)(2,1)S(1)}, bf16[8,48,768]{2,1,0:T(8,128)(2,1)S(1)}, u32[]{:S(2)}, u32[]{:S(2)}) collective-permute-start(bf16[8,48,768]{2,1,0:T(8,128)(2,1)S(1)} %constant_dynamic-update-slice_fusion.28.w2), channel_id=1, source_target_pairs={{0,2},{1,3},{2,0},{3,1},{4,6},{5,7},{6,4},{7,5},{8,10},{9,11},{10,... | collective-permute-start | bytes 1769480 | tf_op jit(solution)/shard_map/ppermute | solution.py:252
  107.1 1.4 collective-permute-start.16
  112.7 20.6 %collective-permute-start.35 = (bf16[8,48,768]{2,1,0:T(8,128)(2,1)S(1)}, bf16[8,48,768]{2,1,0:T(8,128)(2,1)S(1)}, u32[]{:S(2)}, u32[]{:S(2)}) collective-permute-start(bf16[8,48,768]{2,1,0:T(8,128)(2,1)S(1)} %get-tuple-element.151), channel_id=1, source_target_pairs={{0,16},{1,17},{2,18},{3,19},{4,20},{5,21},{6,22},{7,23},{8,24},{9,... | collective-permute-start | bytes 1769480 | tf_op jit(solution)/shard_map/ppermute | solution.py:252
  114.3 20.7 %collective-permute-start.37 = (bf16[8,48,768]{2,1,0:T(8,128)(2,1)S(1)}, bf16[8,48,768]{2,1,0:T(8,128)(2,1)S(1)}, u32[]{:S(2)}, u32[]{:S(2)}) collective-permute-start(bf16[8,48,768]{2,1,0:T(8,128)(2,1)S(1)} %get-tuple-element.153), channel_id=1, source_target_pairs={{0,2},{1,3},{2,0},{3,1},{4,6},{5,7},{6,4},{7,5},{8,10},{9,11},{10,... | collective-permute-start | bytes 1769480 | tf_op jit(solution)/shard_map/ppermute | solution.py:252
  125.9 10.7 %collective-permute-start.29 = (bf16[512,768]{1,0:T(8,128)(2,1)S(1)}, bf16[512,768]{1,0:T(8,128)(2,1)S(1)}, u32[]{:S(2)}, u32[]{:S(2)}) collective-permute-start(bf16[512,768]{1,0:T(8,128)(2,1)S(1)} %get-tuple-element.118.part_mine), channel_id=1, source_target_pairs={{0,1},{1,0},{2,3},{3,2},{4,5},{5,4},{6,7},{7,6},{8,9},{9,8},{10,11... | collective-permute-start | bytes 2359304 | tf_op jit(solution)/shard_map/ppermute | solution.py:252
  126.0 22.5 %collective-permute-start.30 = (bf16[8,48,768]{2,1,0:T(8,128)(2,1)S(1)}, bf16[8,48,768]{2,1,0:T(8,128)(2,1)S(1)}, u32[]{:S(2)}, u32[]{:S(2)}) collective-permute-start(bf16[8,48,768]{2,1,0:T(8,128)(2,1)S(1)} %get-tuple-element.130), channel_id=1, source_target_pairs={{0,16},{1,17},{2,18},{3,19},{4,20},{5,21},{6,22},{7,23},{8,24},{9,... | collective-permute-start | bytes 1769480 | tf_op jit(solution)/shard_map/ppermute | solution.py:252
  127.5 21.0 %collective-permute-start.31 = (bf16[8,48,768]{2,1,0:T(8,128)(2,1)S(1)}, bf16[8,48,768]{2,1,0:T(8,128)(2,1)S(1)}, u32[]{:S(2)}, u32[]{:S(2)}) collective-permute-start(bf16[8,48,768]{2,1,0:T(8,128)(2,1)S(1)} %get-tuple-element.132), channel_id=1, source_target_pairs={{0,2},{1,3},{2,0},{3,1},{4,6},{5,7},{6,4},{7,5},{8,10},{9,11},{10,... | collective-permute-start | bytes 1769480 | tf_op jit(solution)/shard_map/ppermute | solution.py:252
  133.4 21.6 %collective-permute-start.36 = (bf16[4,48,768]{2,1,0:T(8,128)(2,1)S(1)}, bf16[4,48,768]{2,1,0:T(8,128)(2,1)S(1)}, u32[]{:S(2)}, u32[]{:S(2)}) collective-permute-start(bf16[4,48,768]{2,1,0:T(8,128)(2,1)S(1)} %add_convert_fusion.9), channel_id=1, source_target_pairs={{0,2},{1,3},{2,0},{3,1},{4,6},{5,7},{6,4},{7,5},{8,10},{9,11},{10,... | collective-permute-start | bytes 884744 | tf_op jit(solution)/shard_map/ppermute | solution.py:252
  135.0 20.2 %collective-permute-start.38 = (bf16[4,48,768]{2,1,0:T(8,128)(2,1)S(1)}, bf16[4,48,768]{2,1,0:T(8,128)(2,1)S(1)}, u32[]{:S(2)}, u32[]{:S(2)}) collective-permute-start(bf16[4,48,768]{2,1,0:T(8,128)(2,1)S(1)} %add_convert_fusion.7), channel_id=1, source_target_pairs={{0,16},{1,17},{2,18},{3,19},{4,20},{5,21},{6,22},{7,23},{8,24},{9,... | collective-permute-start | bytes 884744 | tf_op jit(solution)/shard_map/ppermute | solution.py:252
  149.5 10.1 %collective-permute-start.34 = (bf16[4,48,768]{2,1,0:T(8,128)(2,1)S(1)}, bf16[4,48,768]{2,1,0:T(8,128)(2,1)S(1)}, u32[]{:S(2)}, u32[]{:S(2)}) collective-permute-start(bf16[4,48,768]{2,1,0:T(8,128)(2,1)S(1)} %add_convert_fusion.10), channel_id=1, source_target_pairs={{0,16},{1,17},{2,18},{3,19},{4,20},{5,21},{6,22},{7,23},{8,24},{9,... | collective-permute-start | bytes 884744 | tf_op jit(solution)/shard_map/ppermute | solution.py:252
  150.0 11.0 %collective-permute-start.33 = (bf16[4,48,768]{2,1,0:T(8,128)(2,1)S(1)}, bf16[4,48,768]{2,1,0:T(8,128)(2,1)S(1)}, u32[]{:S(2)}, u32[]{:S(2)}) collective-permute-start(bf16[4,48,768]{2,1,0:T(8,128)(2,1)S(1)} %add_convert_fusion.11), channel_id=1, source_target_pairs={{0,2},{1,3},{2,0},{3,1},{4,6},{5,7},{6,4},{7,5},{8,10},{9,11},{10,... | collective-permute-start | bytes 884744 | tf_op jit(solution)/shard_map/ppermute | solution.py:252
  151.0 10.0 %collective-permute-start.32 = (bf16[8,2,64,768]{3,2,1,0:T(8,128)(2,1)S(1)}, bf16[8,2,64,768]{3,2,1,0:T(8,128)(2,1)S(1)}, u32[]{:S(2)}, u32[]{:S(2)}) collective-permute-start(bf16[8,2,64,768]{3,2,1,0:T(8,128)(2,1)S(1)} %get-tuple-element.134), channel_id=1, source_target_pairs={{0,1},{1,0},{2,3},{3,2},{4,5},{5,4},{6,7},{7,6},{8,9},{9,8},{10,11... | collective-permute-start | bytes 4718600 | tf_op jit(solution)/shard_map/ppermute | solution.py:252
  155.3 8.1 %slice-start = ((bf16[8,48,768]{2,1,0:T(8,128)(2,1)}), bf16[4,48,768]{2,1,0:T(8,128)(2,1)S(1)}, s32[]{:S(2)}) async-start(bf16[8,48,768]{2,1,0:T(8,128)(2,1)} %copy-done.1), calls=%async_computation | async-start | bytes 589824 | tf_op jit(solution)/shard_map/slice | solution.py:340
  155.3 17.4 %collective-permute-start.41 = (bf16[48,1536]{1,0:T(8,128)(2,1)S(1)}, bf16[48,1536]{1,0:T(8,128)(2,1)S(1)}, u32[]{:S(2)}, u32[]{:S(2)}) collective-permute-start(bf16[48,1536]{1,0:T(8,128)(2,1)S(1)} %get-tuple-element.211), channel_id=1, source_target_pairs={{0,12},{1,13},{2,14},{3,15},{4,8},{5,9},{6,10},{7,11},{8,4},{9,5},... | collective-permute-start | bytes 442376 | tf_op jit(solution)/shard_map/ppermute | solution.py:252
  159.6 16.1 %collective-permute-start.39 = (bf16[48,1536]{1,0:T(8,128)(2,1)S(1)}, bf16[48,1536]{1,0:T(8,128)(2,1)S(1)}, u32[]{:S(2)}, u32[]{:S(2)}) collective-permute-start(bf16[48,1536]{1,0:T(8,128)(2,1)S(1)} %get-tuple-element.213), channel_id=1, source_target_pairs={{0,4},{1,5},{2,6},{3,7},{4,0},{5,1},{6,2},{7,3},{8,12},{9,13},{10,... | collective-permute-start | bytes 442376 | tf_op jit(solution)/shard_map/ppermute | solution.py:252
  159.6 18.4 %collective-permute-start.40 = (bf16[48,1536]{1,0:T(8,128)(2,1)S(1)}, bf16[48,1536]{1,0:T(8,128)(2,1)S(1)}, u32[]{:S(2)}, u32[]{:S(2)}) collective-permute-start(bf16[48,1536]{1,0:T(8,128)(2,1)S(1)} %get-tuple-element.214), channel_id=1, source_target_pairs={{0,8},{1,9},{2,10},{3,11},{4,12},{5,13},{6,14},{7,15},{8,0},{9,1},... | collective-permute-start | bytes 442376 | tf_op jit(solution)/shard_map/ppermute | solution.py:252
  161.0 10.0 %collective-permute-start.51 = (bf16[8,48,384]{2,1,0:T(8,128)(2,1)S(1)}, bf16[8,48,384]{2,1,0:T(8,128)(2,1)S(1)}, u32[]{:S(2)}, u32[]{:S(2)}) collective-permute-start(bf16[8,48,384]{2,1,0:T(8,128)(2,1)S(1)} %get-tuple-element.165), channel_id=1, source_target_pairs={{0,2},{1,3},{2,0},{3,1},{4,6},{5,7},{6,4},{7,5},{8,10},{9,11},{10,... | collective-permute-start | bytes 884744 | tf_op jit(solution)/shard_map/ppermute | solution.py:252
  162.7 23.3 %collective-permute-start.45 = (bf16[4,2,64,768]{3,2,1,0:T(8,128)(2,1)S(1)}, bf16[4,2,64,768]{3,2,1,0:T(8,128)(2,1)S(1)}, u32[]{:S(2)}, u32[]{:S(2)}) collective-permute-start(bf16[4,2,64,768]{3,2,1,0:T(8,128)(2,1)S(1)} %add_convert_fusion.1), channel_id=1, source_target_pairs={{0,2},{1,3},{2,0},{3,1},{4,6},{5,7},{6,4},{7,5},{8,10},{9,11},{10,... | collective-permute-start | bytes 2359304 | tf_op jit(solution)/shard_map/ppermute | solution.py:252
  171.1 5.2 %collective-permute-start.52 = (bf16[4,48,384]{2,1,0:T(8,128)(2,1)S(1)}, bf16[4,48,384]{2,1,0:T(8,128)(2,1)S(1)}, u32[]{:S(2)}, u32[]{:S(2)}) collective-permute-start(bf16[4,48,384]{2,1,0:T(8,128)(2,1)S(1)} %add_convert_fusion.13), channel_id=1, source_target_pairs={{0,16},{1,17},{2,18},{3,19},{4,20},{5,21},{6,22},{7,23},{8,24},{9,... | collective-permute-start | bytes 442376 | tf_op jit(solution)/shard_map/ppermute | solution.py:252
  172.7 7.9 %collective-permute-start.44 = (bf16[48,1536]{1,0:T(8,128)(2,1)S(1)}, bf16[48,1536]{1,0:T(8,128)(2,1)S(1)}, u32[]{:S(2)}, u32[]{:S(2)}) collective-permute-start(bf16[48,1536]{1,0:T(8,128)(2,1)S(1)} %get-tuple-element.207), channel_id=1, source_target_pairs={{0,12},{1,13},{2,14},{3,15},{4,8},{5,9},{6,10},{7,11},{8,4},{9,5},... | collective-permute-start | bytes 442376 | tf_op jit(solution)/shard_map/ppermute | solution.py:252
  175.7 6.6 %collective-permute-start.42 = (bf16[48,1536]{1,0:T(8,128)(2,1)S(1)}, bf16[48,1536]{1,0:T(8,128)(2,1)S(1)}, u32[]{:S(2)}, u32[]{:S(2)}) collective-permute-start(bf16[48,1536]{1,0:T(8,128)(2,1)S(1)} %get-tuple-element.209), channel_id=1, source_target_pairs={{0,4},{1,5},{2,6},{3,7},{4,0},{5,1},{6,2},{7,3},{8,12},{9,13},{10,... | collective-permute-start | bytes 442376 | tf_op jit(solution)/shard_map/ppermute | solution.py:252
  176.3 9.4 %collective-permute-start.43 = (bf16[48,1536]{1,0:T(8,128)(2,1)S(1)}, bf16[48,1536]{1,0:T(8,128)(2,1)S(1)}, u32[]{:S(2)}, u32[]{:S(2)}) collective-permute-start(bf16[48,1536]{1,0:T(8,128)(2,1)S(1)} %get-tuple-element.210), channel_id=1, source_target_pairs={{0,8},{1,9},{2,10},{3,11},{4,12},{5,13},{6,14},{7,15},{8,0},{9,1},... | collective-permute-start | bytes 442376 | tf_op jit(solution)/shard_map/ppermute | solution.py:252
  178.0 18.2 %collective-permute-start.49 = (bf16[8,48,1152]{2,1,0:T(8,128)(2,1)S(1)}, bf16[8,48,1152]{2,1,0:T(8,128)(2,1)S(1)}, u32[]{:S(2)}, u32[]{:S(2)}) collective-permute-start(bf16[8,48,1152]{2,1,0:T(8,128)(2,1)S(1)} %get-tuple-element.163), channel_id=1, source_target_pairs={{0,16},{1,17},{2,18},{3,19},{4,20},{5,21},{6,22},{7,23},{8,24},{9,... | collective-permute-start | bytes 2654216 | tf_op jit(solution)/shard_map/ppermute | solution.py:252
  187.2 34.4 %collective-permute-start.48 = (bf16[2,64,768]{2,1,0:T(8,128)(2,1)}, bf16[2,64,768]{2,1,0:T(8,128)(2,1)S(1)}, u32[]{:S(2)}, u32[]{:S(2)}) collective-permute-start(bf16[2,64,768]{2,1,0:T(8,128)(2,1)} %get-tuple-element.200), channel_id=1, source_target_pairs={{8,4},{9,5},{10,6},{11,7},{12,0},{13,1},{14,2},{15,3},{24,20},{25,... | collective-permute-start | bytes 589832 | tf_op jit(solution)/shard_map/ppermute | solution.py:252
  188.4 33.1 %collective-permute-start.47 = (bf16[2,64,768]{2,1,0:T(8,128)(2,1)}, bf16[2,64,768]{2,1,0:T(8,128)(2,1)S(1)}, u32[]{:S(2)}, u32[]{:S(2)}) collective-permute-start(bf16[2,64,768]{2,1,0:T(8,128)(2,1)} %get-tuple-element.201), channel_id=1, source_target_pairs={{8,0},{9,1},{10,2},{11,3},{12,4},{13,5},{14,6},{15,7},{24,16},{25,... | collective-permute-start | bytes 589832 | tf_op jit(solution)/shard_map/ppermute | solution.py:252
  190.0 8.8 %collective-permute-start.57 = (f32[24,1536]{1,0:T(8,128)S(1)}, f32[24,1536]{1,0:T(8,128)S(1)}, u32[]{:S(2)}, u32[]{:S(2)}) collective-permute-start(f32[24,1536]{1,0:T(8,128)S(1)} %broadcast_select_fusion.6), channel_id=1, source_target_pairs={{0,1},{1,0},{2,3},{3,2},{4,5},{5,4},{6,7},{7,6},{8,9},{9,8},{10,11... | collective-permute-start | bytes 442376 | tf_op jit(solution)/shard_map/ppermute | solution.py:252
  197.2 8.6 %collective-permute-start.50 = (bf16[4,48,1152]{2,1,0:T(8,128)(2,1)}, bf16[4,48,1152]{2,1,0:T(8,128)(2,1)}, u32[]{:S(2)}, u32[]{:S(2)}) collective-permute-start(bf16[4,48,1152]{2,1,0:T(8,128)(2,1)} %add_convert_fusion.3), channel_id=1, source_target_pairs={{0,2},{1,3},{2,0},{3,1},{4,6},{5,7},{6,4},{7,5},{8,10},{9,11},{10,... | collective-permute-start | bytes 1327112 | tf_op jit(solution)/shard_map/ppermute | solution.py:252
  200.8 6.3 %copy-start = (f32[24,3072]{1,0:T(8,128)}, f32[24,3072]{1,0:T(8,128)S(1)}, u32[]{:S(2)}) copy-start(f32[24,3072]{1,0:T(8,128)S(1)} %reshape.60) | copy-start | bytes 884740
  200.8 10.3 %copy-start.11 = (bf16[24]{0:T(256)(128)(2,1)S(1)}, bf16[24]{0:T(256)(128)(2,1)}, u32[]{:S(2)}) copy-start(bf16[24]{0:T(256)(128)(2,1)} %param.17) | copy-start | bytes 148
  200.8 13.0 %copy-start.7 = (bf16[2,64,768]{2,1,0:T(8,128)(2,1)S(1)}, bf16[2,64,768]{2,1,0:T(8,128)(2,1)}, u32[]{:S(2)}) copy-start(bf16[2,64,768]{2,1,0:T(8,128)(2,1)} %get-tuple-element.202) | copy-start | bytes 589828
  207.1 6.6 %collective-permute-start.53 = (bf16[48,1536]{1,0:T(8,128)(2,1)S(1)}, bf16[48,1536]{1,0:T(8,128)(2,1)S(1)}, u32[]{:S(2)}, u32[]{:S(2)}) collective-permute-start(bf16[48,1536]{1,0:T(8,128)(2,1)S(1)} %get-tuple-element.204), channel_id=1, source_target_pairs={{0,4},{1,5},{2,6},{3,7},{4,0},{5,1},{6,2},{7,3},{8,12},{9,13},{10,... | collective-permute-start | bytes 442376 | tf_op jit(solution)/shard_map/ppermute | solution.py:252
  208.8 9.7 %collective-permute-start.55 = (bf16[48,1536]{1,0:T(8,128)(2,1)S(1)}, bf16[48,1536]{1,0:T(8,128)(2,1)S(1)}, u32[]{:S(2)}, u32[]{:S(2)}) collective-permute-start(bf16[48,1536]{1,0:T(8,128)(2,1)S(1)} %get-tuple-element.205), channel_id=1, source_target_pairs={{0,12},{1,13},{2,14},{3,15},{4,8},{5,9},{6,10},{7,11},{8,4},{9,5},... | collective-permute-start | bytes 442376 | tf_op jit(solution)/shard_map/ppermute | solution.py:252
  211.1 10.2 %collective-permute-start.54 = (bf16[48,1536]{1,0:T(8,128)(2,1)S(1)}, bf16[48,1536]{1,0:T(8,128)(2,1)S(1)}, u32[]{:S(2)}, u32[]{:S(2)}) collective-permute-start(bf16[48,1536]{1,0:T(8,128)(2,1)S(1)} %get-tuple-element.206), channel_id=1, source_target_pairs={{0,8},{1,9},{2,10},{3,11},{4,12},{5,13},{6,14},{7,15},{8,0},{9,1},... | collective-permute-start | bytes 442376 | tf_op jit(solution)/shard_map/ppermute | solution.py:252
  213.8 8.5 %collective-permute-start.46 = (bf16[2,64,768]{2,1,0:T(8,128)(2,1)S(1)}, bf16[2,64,768]{2,1,0:T(8,128)(2,1)S(1)}, u32[]{:S(2)}, u32[]{:S(2)}) collective-permute-start(bf16[2,64,768]{2,1,0:T(8,128)(2,1)S(1)} %copy-done.7), channel_id=1, source_target_pairs={{4,0},{5,1},{6,2},{7,3},{12,8},{13,9},{14,10},{15,11},{20,16},{21,... | collective-permute-start | bytes 589832 | tf_op jit(solution)/shard_map/ppermute | solution.py:252
  221.5 2.0 collective-permute-start.56
  (9 other events, 16.7 us)
